TPU v7x, 256 devices: a whole 4x4x8 slice. The times are simulated.
256 devices in a mesh: dp: 2 (over y_lo), ctx: 16 (over y_hi, z), tensor: 8 (over x, core).
Axes of the slice: x: 4, y: 4 (y_hi: 2, y_lo: 2; y = y_hi * 2 + y_lo), z: 8, core: 2. Of those that a mesh axis runs over, the one named last changes fastest.
Arguments:
- input_spikes: int32 [512, 8192], P(None, ('dp', 'ctx')), may hold values from 0 to 65535
- query_spikes: int32 [512, 8192], P('tensor', ('dp', 'ctx')), may hold values from 0 to 65535
- key_spikes: int32 [512, 8192], P('tensor', ('dp', 'ctx')), may hold values from 0 to 65535
- values: bfloat16 [8192, 8192], P(('dp', 'ctx'), 'tensor'), may hold values from -6 to 6
- query_slope: bfloat16 [8192, 8192], P(('dp', 'ctx'), 'tensor'), may hold values from 0.25 to 2
- key_slope: bfloat16 [8192, 8192], P(('dp', 'ctx'), 'tensor'), may hold values from 0.25 to 2
- grad_out: bfloat16 [8192, 8192], P(('dp', 'ctx'), 'tensor'), may hold values from -6 to 6
- log_gate: float32 [64, 8192], P('tensor', ('dp', 'ctx')), may hold values from -0.8 to 0
- pattern: int32 [128, 16], P('tensor'), may hold values from 0 to 127, all different within a row
Outputs:
- query_grad: bfloat16 [8192, 8192], P(('dp', 'ctx'), 'tensor')
- key_grad: bfloat16 [8192, 8192], P(('dp', 'ctx'), 'tensor')
- value_grad: float32 [16, 128, 4096], P('ctx', 'tensor')
Inputs may be any that keep to these rules, and one draw needn't show every extreme that they name: `pattern`: each column block names 16 different row blocks.
All inputs are finite; a program needn't handle non-finite values.
Results may differ from a plain program's by a relative error of at most 0.0073.
Values sent between devices are 32-bit elements; how exact they have to be, the bound alone decides.
A program may use at most 128 MiB of HBM per device.

v0:
```python
import jax
import jax.numpy as jnp
from jax import lax
from jax.sharding import PartitionSpec as P

D = 8192
HEAD = 128
BLK = 64
SEL = 16


highest = lax.Precision.HIGHEST


def entering(value, axis, combine, identity, reverse):
    devices, place = (lax.axis_size(axis), lax.axis_index(axis))
    everything = jax.tree.map(lambda part: lax.all_gather(part, axis), value)
    start = jax.tree.map(
        lambda part, zero: jnp.broadcast_to(jnp.asarray(zero, part.dtype), part.shape),
        value,
        identity,
    )

    def turn(k, before):
        at = devices - 1 - k if reverse else k
        reached = at > place if reverse else at < place
        new = combine(before, jax.tree.map(lambda part: part[at], everything))
        return jax.tree.map(lambda a, b: jnp.where(reached, a, b), new, before)

    return lax.fori_loop(0, devices, turn, start)


def dims_of(left_dim, right_dim):
    return (((left_dim,), (right_dim,)), ((), ()))


def unpack_flags(packed):
    shifts = jnp.arange(16, dtype=jnp.int32)
    flags = jnp.bitwise_and(jnp.right_shift(packed[:, None, :], shifts[None, :, None]), 1)
    return flags.reshape(packed.shape[0] * 16, packed.shape[1]).astype(jnp.bfloat16)


def decay_matrix(cumulative):
    spread = cumulative[:, None] - cumulative[None, :]
    places = jnp.arange(cumulative.shape[0])
    causal = places[:, None] >= places[None, :]
    return jnp.where(causal, jnp.exp(jnp.minimum(spread, 0.0)), 0.0)


def first_phase(query_cols, key_cols, head_values, cumulative):
    decays = decay_matrix(cumulative)
    intersection = lax.dot_general(
        query_cols, key_cols, dims_of(0, 0), preferred_element_type=jnp.float32
    )
    weights = intersection * decays
    weights_low = weights.astype(jnp.bfloat16)
    local_num = jnp.dot(weights_low, head_values, preferred_element_type=jnp.float32)
    local_den = jnp.sum(weights, axis=1)
    tail_decay = jnp.exp(cumulative[-1] - cumulative)
    key_float = key_cols.astype(jnp.float32) * tail_decay[None, :]
    state_sum = jnp.dot(key_float, head_values.astype(jnp.float32), precision=highest)
    key_sum = jnp.sum(key_float, axis=1)
    return (weights_low, local_num, local_den, jnp.exp(cumulative[-1]), state_sum, key_sum)


def second_phase(
    query_cols,
    key_cols,
    head_values,
    head_grad,
    cumulative,
    weights_low,
    local_num,
    local_den,
    state_in,
    keys_in,
):
    decays = decay_matrix(cumulative)
    lead_decay = jnp.exp(cumulative)
    query_float = query_cols.astype(jnp.float32)
    carried_num = lax.dot_general(query_float, state_in, dims_of(0, 0), precision=highest)
    numerator = local_num + lead_decay[:, None] * carried_num
    denominator = 1.0 + local_den + lead_decay * jnp.dot(keys_in, query_float, precision=highest)
    output = numerator / denominator[:, None]
    grad_float = head_grad.astype(jnp.float32)
    scaled = grad_float / denominator[:, None]
    norm_grad = -jnp.sum(grad_float * output, axis=1) / denominator
    scaled_low = scaled.astype(jnp.bfloat16)
    cross_term = lax.dot_general(
        scaled_low, head_values, dims_of(1, 1), preferred_element_type=jnp.float32
    )
    mixed_low = ((cross_term + norm_grad[:, None]) * decays).astype(jnp.bfloat16)
    carried_query = (
        lax.dot_general(scaled, state_in, dims_of(1, 1), precision=highest)
        + norm_grad[:, None] * keys_in[None, :]
    )
    grad_query = (
        lax.dot_general(mixed_low, key_cols, dims_of(1, 1), preferred_element_type=jnp.float32)
        + lead_decay[:, None] * carried_query
    )
    grad_key = lax.dot_general(
        mixed_low, query_cols, dims_of(0, 1), preferred_element_type=jnp.float32
    )
    grad_value = lax.dot_general(
        weights_low, scaled_low, dims_of(0, 0), preferred_element_type=jnp.float32
    )
    adjoint_sum = jnp.dot(query_float * lead_decay[None, :], scaled, precision=highest)
    adjoint_vec = jnp.dot(query_float, lead_decay * norm_grad, precision=highest)
    return (grad_query, grad_key, grad_value, adjoint_sum, adjoint_vec)


def third_phase(
    key_cols, head_values, cumulative, grad_key_local, grad_value_local, adjoint, adjoint_vec
):
    tail_decay = jnp.exp(cumulative[-1] - cumulative)[:, None]
    value_float = head_values.astype(jnp.float32)
    key_float = key_cols.astype(jnp.float32)
    grad_key = grad_key_local + tail_decay * (
        lax.dot_general(value_float, adjoint, dims_of(1, 1), precision=highest)
        + adjoint_vec[None, :]
    )
    grad_value = grad_value_local + tail_decay * lax.dot_general(
        key_float, adjoint, dims_of(0, 0), precision=highest
    )
    return (grad_key, grad_value)


def combine_forward(earlier_part, later_part):
    total_early, state_early, keys_early = earlier_part
    total_late, state_late, keys_late = later_part
    return (
        total_early * total_late,
        total_late[:, None, None] * state_early + state_late,
        total_late[:, None] * keys_early + keys_late,
    )


def combine_backward(earlier_part, later_part):
    total_early, adjoint_early, vector_early = earlier_part
    total_late, adjoint_late, vector_late = later_part
    return (
        total_early * total_late,
        adjoint_late + total_late[:, None, None] * adjoint_early,
        vector_late + total_late[:, None] * vector_early,
    )


def run_first(block_items):
    return first_phase(*block_items)


def run_second(block_items):
    return second_phase(*block_items)


def per_device(
    input_spikes,
    query_spikes,
    key_spikes,
    values,
    query_slope,
    key_slope,
    grad_out,
    log_gate,
    pattern,
):
    tokens_here = values.shape[0]
    heads_here = values.shape[1] // HEAD
    query_cols = unpack_flags(query_spikes).reshape(heads_here, HEAD, tokens_here)
    key_cols = unpack_flags(key_spikes).reshape(heads_here, HEAD, tokens_here)
    head_values = values.reshape(tokens_here, heads_here, HEAD).transpose(1, 0, 2)
    head_grads = grad_out.reshape(tokens_here, heads_here, HEAD).transpose(1, 0, 2)
    cumulative = jnp.cumsum(log_gate, axis=1)
    weights_low, local_num, local_den, totals, state_sum, key_sum = lax.map(
        run_first, (query_cols, key_cols, head_values, cumulative)
    )
    identity_state = (
        jnp.ones((heads_here,), jnp.float32),
        jnp.zeros((heads_here, HEAD, HEAD), jnp.float32),
        jnp.zeros((heads_here, HEAD), jnp.float32),
    )
    carried_state = entering(
        (totals, state_sum, key_sum), "ctx", combine_forward, identity_state, False
    )
    grad_query, grad_key_local, grad_value_local, adjoint_sum, adjoint_vec = lax.map(
        run_second,
        (
            query_cols,
            key_cols,
            head_values,
            head_grads,
            cumulative,
            weights_low,
            local_num,
            local_den,
            carried_state[1],
            carried_state[2],
        ),
    )
    carried_adjoint = entering(
        (totals, adjoint_sum, adjoint_vec), "ctx", combine_backward, identity_state, True
    )
    grad_key, grad_value = jax.vmap(third_phase)(
        key_cols,
        head_values,
        cumulative,
        grad_key_local,
        grad_value_local,
        carried_adjoint[1],
        carried_adjoint[2],
    )
    width_here = heads_here * HEAD
    flat_query = grad_query.transpose(1, 0, 2).reshape(tokens_here, width_here)
    flat_key = grad_key.transpose(1, 0, 2).reshape(tokens_here, width_here)
    query_grad = (query_slope.astype(jnp.float32) * flat_query).astype(jnp.bfloat16)
    key_grad = (key_slope.astype(jnp.float32) * flat_key).astype(jnp.bfloat16)
    column_blocks = pattern.shape[0]
    value_low = grad_value.transpose(1, 0, 2).reshape(tokens_here, width_here).astype(jnp.bfloat16)
    value_blocks = value_low.reshape(tokens_here, column_blocks, BLK)
    input_cols = unpack_flags(input_spikes)
    row_share = SEL // lax.axis_size("ctx")
    input_blocks = input_cols.reshape(D // BLK, BLK, tokens_here)
    chosen = pattern.T
    gathered = jnp.take(input_blocks, chosen, axis=0)
    partial_value = jnp.einsum(
        "snat,tnb->snab", gathered, value_blocks, preferred_element_type=jnp.float32
    )
    reduced = lax.psum_scatter(
        partial_value.reshape(lax.axis_size("ctx") * row_share, column_blocks, BLK * BLK),
        "ctx",
        scatter_dimension=0,
        tiled=True,
    )
    value_grad = lax.psum(reduced, "dp")
    return (query_grad, key_grad, value_grad)


def solution(mesh):
    in_specs = (
        P(None, ("dp", "ctx")),
        P("tensor", ("dp", "ctx")),
        P("tensor", ("dp", "ctx")),
        P(("dp", "ctx"), "tensor"),
        P(("dp", "ctx"), "tensor"),
        P(("dp", "ctx"), "tensor"),
        P(("dp", "ctx"), "tensor"),
        P("tensor", ("dp", "ctx")),
        P("tensor", None),
    )
    out_specs = (P(("dp", "ctx"), "tensor"), P(("dp", "ctx"), "tensor"), P("ctx", "tensor", None))
    return jax.shard_map(
        per_device, mesh=mesh, in_specs=in_specs, out_specs=out_specs, check_vma=False
    )
```

profile of v0, /device:TPU:14, one launch (start us, length us, event | category | flops | bytes accessed | tf_op | source)
XLA Modules:
  0.0 711.3 jit_solution(3989834290211773359)
XLA Ops:
  7.3 1.2 reduce-window.6
  8.9 1.2 copy.49
  12.6 34.4 %while.72 = (s32[]{:T(128)}, bf16[8,256,256]{1,2,0:T(8,128)(2,1)}, f32[8,256,128]{2,1,0:T(8,128)}, f32[8,256]{1,0:T(8,128)S(1)}, f32[8]{0:T(128)S(1)}, /*index=5...) while((s32[]{:T(128)}, bf16[8,256,256]{1,2,0:T(8,128)(2,1)}, ...), condition=%wide.region_5.6_spmd, body=%wide.region_2.5_spmd.sunk | while | flops 84574080 | bytes 1523417 | solution.py:174
  48.0 2.0 copy.48
  51.6 44.3 %all-reduce = f32[128]{0:T(128)S(1)} all-reduce(f32[128]{0:T(128)S(1)} %dynamic-update-slice), channel_id=2, replica_groups=mesh['dp'=2,'ctx'=16,'tensor'=8] {'ctx'}, use_global_device_ids=true, to_apply=%add | all-reduce | flops 128 | bytes 1024
  96.0 36.7 %all-gather.2 = f32[128,128]{1,0:T(8,128)S(1)} all-gather(f32[8,128]{1,0:T(8,128)S(1)} %get-tuple-element.456), channel_id=4, replica_groups=mesh['dp'=2,'ctx'=16,'tensor'=8] {'ctx'}, dimensions={0}, use_global_device_ids=true | all-gather | bytes 69632 | tf_op jit(solution)/shard_map/all_gather | solution.py:17
  132.7 52.9 %all-gather.8.cloned.1.call-done = f32[128,128,128]{2,1,0:T(8,128)} async-done(((f32[8,128,128]{2,1,0:T(8,128)}), f32[128,128,128]{2,1,0:T(8,128)}) %all-gather.8.cloned.1.call-update) | async-done | bytes 8388624 | tf_op jit(solution)/shard_map/all_gather | solution.py:17
  185.6 20.1 %while.74 = (s32[]{:T(128)}, f32[8,128,128]{2,1,0:T(8,128)S(1)}, f32[8,128]{1,0:T(8,128)S(1)}, s32[]{:T(128)}, f32[16,8]{1,0:T(8,128)S(1)}, /*index=5*/f32[16,8,...) while((s32[]{:T(128)}, f32[8,128,128]{2,1,0:T(8,128)S(1)}, ...), condition=%wide.region_7.8_spmd.clone, body=%wide.region_6.7_spmd.clone.sunk | while | flops 528388 | bytes 1585415 | solution.py:30
  185.6 1.2 fusion.185
  186.8 1.2 fusion.185
  188.1 1.2 fusion.185
  189.3 1.2 fusion.185
  190.6 1.2 fusion.185
  191.9 1.2 fusion.185
  193.1 1.2 fusion.185
  194.4 1.2 fusion.185
  195.6 1.2 fusion.185
  196.9 1.2 fusion.185
  198.1 1.2 fusion.185
  199.4 1.2 fusion.185
  200.6 1.2 fusion.185
  201.9 1.2 fusion.185
  203.2 1.2 fusion.185
  204.4 1.2 fusion.185
  205.7 75.2 %while.73 = (s32[]{:T(128)}, f32[8,256,128]{1,2,0:T(8,128)}, f32[8,256,128]{1,2,0:T(8,128)}, f32[8,256,128]{1,2,0:T(8,128)}, f32[8,128,128]{2,1,0:T(8,128)S(1)},...) while((s32[]{:T(128)}, f32[8,256,128]{1,2,0:T(8,128)}, ...), condition=%wide.region_10.11_spmd, body=%wide.region_8.10_spmd.sunk | while | flops 220071168 | bytes 2862273 | solution.py:185
  212.0 1.8 fusion.181
  221.4 1.8 fusion.181
  230.8 1.8 fusion.181
  240.2 1.8 fusion.181
  249.6 1.8 fusion.181
  259.0 1.8 fusion.181
  268.4 1.8 fusion.181
  277.8 1.8 fusion.181
  282.2 1.7 shift_right_arithmetic.72
  283.9 3.7 fusion.81
  287.7 10.9 %gather_fusion = bf16[256,64,256]{2,1,0:T(8,128)(2,1)} fusion(bf16[128,64,256]{2,1,0:T(8,128)(2,1)} %fusion.81, s32[1024]{0:T(1024)S(1)} %pad_clamp_fusion), kind=kCustom, calls=%fused_computation | custom fusion | bytes 16778240 | tf_op jit(solution)/shard_map/jit(_take)/gather | solution.py:224
  298.8 37.9 %all-gather.4 = f32[128,128]{1,0:T(8,128)S(1)} all-gather(f32[8,128]{1,0:T(8,128)S(1)} %get-tuple-element.464), channel_id=6, replica_groups=mesh['dp'=2,'ctx'=16,'tensor'=8] {'ctx'}, dimensions={0}, use_global_device_ids=true | all-gather | bytes 69632 | tf_op jit(solution)/shard_map/all_gather | solution.py:17
  336.7 76.9 %all-gather.10.cloned.1.call-done = f32[128,128,128]{2,1,0:T(8,128)} async-done(((f32[8,128,128]{2,1,0:T(8,128)}), f32[128,128,128]{2,1,0:T(8,128)}) %all-gather.10.cloned.1.call-update) | async-done | bytes 8388624 | tf_op jit(solution)/shard_map/all_gather | solution.py:17
  413.6 20.1 %while.75 = (s32[]{:T(128)}, f32[8,128,128]{2,1,0:T(8,128)S(1)}, f32[8,128]{1,0:T(8,128)S(1)}, s32[]{:T(128)}, f32[16,8,128,128]{3,2,1,0:T(8,128)}, /*index=5*/f...) while((s32[]{:T(128)}, f32[8,128,128]{2,1,0:T(8,128)S(1)}, ...), condition=%wide.region_12.13_spmd.clone, body=%wide.region_11.12_spmd.clone.sunk | while | flops 528392 | bytes 1585477 | solution.py:30
  413.6 1.2 fusion.188
  414.8 1.2 fusion.188
  416.1 1.2 fusion.188
  417.4 1.2 fusion.188
  418.6 1.2 fusion.188
  419.9 1.2 fusion.188
  421.1 1.2 fusion.188
  422.4 1.2 fusion.188
  423.6 1.2 fusion.188
  424.9 1.2 fusion.188
  426.1 1.2 fusion.188
  427.4 1.2 fusion.188
  428.6 1.2 fusion.188
  429.9 1.2 fusion.188
  431.2 1.2 fusion.188
  432.4 1.2 fusion.188
  434.3 8.6 %fusion.84 = f32[16,16,64,64]{2,3,0,1:T(8,128)} fusion(bf16[256,16,64,1]{0,2,3,1:T(8,128)(2,1)S(1)} %bitcast.307, bf16[16,16,64,256]{3,2,1,0:T(8,128)(2,1)} %bitcast.298, pred[16,16]{1,0:T(8,128)(4,1)S(1)} %copy.63), kind=kOutput, calls=%fused_computation.118 | convolution fusion | flops 541065216 | bytes 13107456 | tf_op jit(solution)/shard_map/snat,tnb->snab/dot_general | solution.py:225
  442.9 9.3 %copy.66 = f32[16,16,64,64]{3,2,1,0:T(8,128)} copy(f32[16,16,64,64]{2,3,0,1:T(8,128)} %fusion.84) | data formatting | bytes 8388608 | tf_op jit(solution)/shard_map/snat,tnb->snab/transpose | solution.py:225
  452.2 8.0 %reshape.163 = f32[16,16,4096]{2,1,0:T(8,128)} reshape(f32[16,16,64,64]{3,2,1,0:T(8,128)} %copy.66) | data formatting | bytes 8388608 | tf_op jit(solution)/shard_map/reshape | solution.py:229
  460.3 1.3 copy.72
  461.6 1.9 fusion.90
  463.8 203.9 %reduce-scatter.2.cloned.1.call-done = f32[1,16,4096]{2,1,0:T(8,128)} async-done(((f32[16,16,4096]{2,1,0:T(8,128)}), f32[1,16,4096]{2,1,0:T(8,128)}) %reduce-scatter.2.cloned.1.call-update) | async-done | bytes 262160 | tf_op jit(solution)/shard_map/reduce_scatter | solution.py:228
  667.7 2.7 multiply_convert_fusion
  670.3 32.8 %all-reduce.3.cloned.1.call-done = f32[1,16,4096]{2,1,0:T(8,128)} async-done(((f32[1,16,4096]{2,1,0:T(8,128)}), f32[1,16,4096]{2,1,0:T(8,128)}) %all-reduce.3.cloned.1.call-update) | async-done | bytes 262160 | tf_op jit(solution)/shard_map/psum | solution.py:234
  703.1 1.7 copy.160
  (327 shorter events, 98.8 us)
Async XLA Ops:
  7.2 178.4 %all-gather.8.cloned.1.call-start = ((), (), s32[]{:S(2)}) async-start(), calls=%async_computation.3 | async-start | bytes 8912896 | tf_op jit(solution)/shard_map/all_gather | solution.py:17
  10.1 39.9 %copy-start.6 = (u32[256]{0:T(256)S(1)}, u32[256]{0:T(256)}, u32[]{:S(2)}) copy-start(u32[256]{0:T(256)} %constant.157) | copy-start | bytes 3076
  47.0 0.8 copy-start
  47.9 365.7 %all-gather.10.cloned.1.call-start = ((), (), s32[]{:S(2)}) async-start(), calls=%async_computation.4 | async-start | bytes 8912896 | tf_op jit(solution)/shard_map/all_gather | solution.py:17
  205.7 76.2 %copy-start.5 = (s32[16,16]{1,0:T(8,128)S(1)}, s32[16,16]{1,0:T(8,128)}, u32[]{:S(2)}) copy-start(s32[16,16]{1,0:T(8,128)} %param.25) | copy-start | bytes 3076
  280.9 0.8 copy-start.1
  281.7 385.9 %reduce-scatter.2.cloned.1.call-start = ((), (), s32[]{:S(2)}) async-start(), calls=%async_computation.1 | async-start | bytes 4456448 | tf_op jit(solution)/shard_map/reduce_scatter | solution.py:228
  287.7 146.0 %copy-start.3 = (f32[8,256,128]{1,2,0:T(8,128)S(1)}, f32[8,256,128]{1,2,0:T(8,128)}, u32[]{:S(2)}) copy-start(f32[8,256,128]{1,2,0:T(8,128)} %get-tuple-element.467) | copy-start | bytes 3145732
  452.2 8.1 %copy-start.2 = (f32[8,256,128]{1,2,0:T(8,128)S(1)}, f32[8,256,128]{1,2,0:T(8,128)}, u32[]{:S(2)}) copy-start(f32[8,256,128]{1,2,0:T(8,128)} %get-tuple-element.461) | copy-start | bytes 3145732
  460.2 207.5 %copy-start.4 = (bf16[256,1024]{1,0:T(8,128)(2,1)S(1)}, bf16[256,1024]{1,0:T(8,128)(2,1)}, u32[]{:S(2)}) copy-start(bf16[256,1024]{1,0:T(8,128)(2,1)} %param.22) | copy-start | bytes 1572868
  460.2 242.9 %all-reduce.3.cloned.1.call-start = ((), (), s32[]{:S(2)}) async-start(), calls=%async_computation.2 | async-start | bytes 524288 | tf_op jit(solution)/shard_map/psum | solution.py:234
Sparse Core Ops, SparseCore 0:
  48.0 137.5 all-gather.7
  281.8 131.6 all-gather.9
  460.3 207.2 reduce-scatter.1
  670.1 32.9 all-reduce.2
where the time goes:
time: 717 us; the launch traced here: 711 us
  waiting for transfers between devices  367 us (51%)
  blocking collectives  119 us (17%)
  matrix products  92.2 us (13%)
  local copies, waits for them, and re-layouts  57.3 us (8%)
  other arithmetic  54.8 us (8%)
  between operations  14.8 us (2%)
    reduce_scatter x1, waiting for transfers between devices, per_device(): lax.psum_scatter(partial_value.reshape(lax.axis_size('ctx') * row_share,...  204 us
    all_gather x2, waiting for transfers between devices, entering(): everything = jax.tree.map(lambda part: lax.all_gather(part, axis), value)  130 us
    all_gather x2, blocking collectives, entering(): everything = jax.tree.map(lambda part: lax.all_gather(part, axis), value)  74.6 us
    unnamed x1, blocking collectives  44.3 us
    select_n x64, other arithmetic, turn(): return jax.tree.map(lambda a, b: jnp.where(reached, a, b), new, before)  39.8 us
    psum x1, waiting for transfers between devices, per_device(): value_grad = lax.psum(reduced, 'dp')  32.8 us
  transfers between devices with their start and end apart: 4, of which 4 were waited for; matrix products, arithmetic and copies ran while one was open for 4% of the time, Pallas kernels for 0%

commit v1 on v0

v1 whole, which is shorter than its diff:
```python
import functools

import jax
import jax.numpy as jnp
from jax import lax
from jax.experimental import pallas as pl
from jax.experimental.pallas import tpu as pltpu
from jax.sharding import PartitionSpec as P

HEAD = 128
BLK = 64
SEL = 16
MESH = pl.DeviceIdType.MESH
CHUNK = 32
HOP = 5
f32 = jnp.float32
bf16 = jnp.bfloat16


def mm(a, b):
    return lax.dot_general(a, b, (((1,), (0,)), ((), ())), preferred_element_type=f32)


def mm_nt(a, b):
    return lax.dot_general(a, b, (((1,), (1,)), ((), ())), preferred_element_type=f32)


def mm_tn(a, b):
    return lax.dot_general(a, b, (((0,), (0,)), ((), ())), preferred_element_type=f32)


def split(a):
    high = a.astype(bf16)
    return high, (a - high.astype(f32)).astype(bf16)


def mm_exact_left(a, b):
    high, low = split(b)
    return mm(a, high) + mm(a, low)


def bits_of(words, tokens):
    spread = jnp.broadcast_to(words[:, None, :], (HEAD // 16, 16, tokens))
    shifts = lax.broadcasted_iota(jnp.int32, spread.shape, 1)
    flags = jnp.bitwise_and(jnp.right_shift(spread, shifts), 1)
    return flags.reshape(HEAD, tokens).astype(f32).astype(bf16)


def enter(partners):
    barrier = pltpu.get_barrier_semaphore()
    for device in partners:
        pl.semaphore_signal(barrier, inc=1, device_id=device, device_id_type=MESH)
    pl.semaphore_wait(barrier, len(partners))


def attention_kernel(
    n, heads, tokens,
    qw, kw, v, do, gate, qs, ks,
    dq, dk, dv,
    kc, kr, qr, lead, tail, wl, num, rden, gl, gf, decay, dvl,
    yy, s_in, s_out, xx, c_in, c_out,
    send1, ag1, send2, ag2, p_rows,
    s1_send, s1_recv, s2_send, s2_recv, f_send, f_recv, b_send, b_recv,
):
    me = lax.axis_index("ctx")
    chunks = heads * HEAD // CHUNK

    barrier = pltpu.get_barrier_semaphore()

    def greet(i, _):
        pl.semaphore_signal(
            barrier, inc=1, device_id={"ctx": lax.rem(me + i, n)}, device_id_type=MESH
        )
        return 0

    lax.fori_loop(1, n, greet, 0)

    rows = lax.broadcasted_iota(jnp.int32, (tokens, tokens), 0)
    cols = lax.broadcasted_iota(jnp.int32, (tokens, tokens), 1)
    lower = (rows >= cols).astype(f32)
    hi = lax.Precision.HIGHEST
    gates = gate[...]
    run_rows = lax.dot_general(
        gates, lower, (((1,), (1,)), ((), ())), precision=hi, preferred_element_type=f32
    )
    p_rows[0:heads, :] = jnp.exp(
        jnp.broadcast_to(jnp.sum(gates, axis=1, keepdims=True), (heads, HEAD))
    )

    def head_cols(h):
        return pl.ds(pl.multiple_of(h * HEAD, HEAD), HEAD)

    def sums(h, _):
        words = pl.ds(pl.multiple_of(h * (HEAD // 16), HEAD // 16), HEAD // 16)
        keys = bits_of(kw[words, :], tokens)
        kc[h] = keys
        key_rows = keys.T
        kr[h] = key_rows
        qr[h] = bits_of(qw[words, :], tokens).T
        spread = jnp.broadcast_to(gate[pl.ds(h, 1), :], (HEAD, tokens))
        run = lax.dot_general(
            lower, spread, (((1,), (1,)), ((), ())), precision=hi, preferred_element_type=f32
        )
        lead[h] = run
        last = jnp.broadcast_to(run[tokens - 1 : tokens, :], (tokens, HEAD))
        end = jnp.exp(last - run)
        tail[h] = end
        send1[pl.ds(h, 1), :] = jnp.sum(key_rows.astype(f32) * end, axis=0, keepdims=True)
        return 0

    lax.fori_loop(0, heads, sums, 0)
    send1[heads : 2 * heads, :] = p_rows[0:heads, :]
    ag1[me] = send1[...]
    pl.semaphore_wait(barrier, n - 1)

    def gather(send, target, send_sem, recv_sem, i):
        peer = lax.rem(me + i, n)
        return pltpu.make_async_remote_copy(
            src_ref=send,
            dst_ref=target.at[me],
            send_sem=send_sem.at[i],
            recv_sem=recv_sem.at[me],
            device_id={"ctx": peer},
            device_id_type=MESH,
        )

    def arrival(send, target, send_sem, recv_sem, i):
        peer = lax.rem(me + i, n)
        return pltpu.make_async_remote_copy(
            src_ref=send,
            dst_ref=target.at[peer],
            send_sem=send_sem.at[i],
            recv_sem=recv_sem.at[peer],
            device_id={"ctx": peer},
            device_id_type=MESH,
        )

    def start_gather(send, target, send_sem, recv_sem):
        def one(i, _):
            gather(send, target, send_sem, recv_sem, i).start()
            return 0

        lax.fori_loop(1, n, one, 0)

    def end_gather(send, target, send_sem, recv_sem):
        def one(i, _):
            arrival(send, target, send_sem, recv_sem, i).wait_recv()
            return 0

        lax.fori_loop(1, n, one, 0)

    def sent_gather(send, target, send_sem, recv_sem):
        def one(i, _):
            gather(send, target, send_sem, recv_sem, i).wait_send()
            return 0

        lax.fori_loop(1, n, one, 0)

    first = (send1, ag1, s1_send, s1_recv)
    second = (send2, ag2, s2_send, s2_recv)
    start_gather(*first)

    def local_part(h, _):
        run = lead[h]
        run_wide = jnp.concatenate([run, run], axis=1)
        run_row = lax.dot_general(
            jnp.broadcast_to(gate[pl.ds(h, 1), :], (8, tokens)), lower,
            (((1,), (1,)), ((), ())), precision=hi, preferred_element_type=f32,
        )[0:1, :]
        spread = run_wide - jnp.broadcast_to(run_row, (tokens, tokens))
        mask = jnp.where(rows >= cols, jnp.exp(jnp.minimum(spread, 0.0)), 0.0)
        decay[h] = mask
        weights = mm(qr[h], kc[h]) * mask
        low = weights.astype(bf16)
        wl[h] = low
        vh = v[:, head_cols(h)]
        num[h] = mm(low, vh)
        rden[h] = jnp.broadcast_to(jnp.sum(weights, axis=1, keepdims=True), (tokens, HEAD))
        yy[h] = mm_exact_left(kc[h], tail[h] * vh.astype(f32))
        lead[h] = jnp.exp(run)
        return 0

    lax.fori_loop(0, heads, local_part, 0)
    end_gather(*first)

    def carry_keys(i, state):
        item = ag1[i]
        new = item[heads : 2 * heads, :] * state + item[0:heads, :]
        return jnp.where(i < me, new, state)

    send2[...] = lax.fori_loop(0, n, carry_keys, jnp.zeros((heads, HEAD), f32))

    def scaled_part(h, _):
        keys_in = jnp.broadcast_to(send2[pl.ds(h, 1), :], (HEAD, HEAD))
        high, low = split(keys_in)
        q_rows = qr[h]
        met = mm_nt(q_rows, high) + mm_nt(q_rows, low)
        inverse = 1.0 / (1.0 + rden[h] + lead[h] * met)
        rden[h] = inverse
        scaled = do[:, head_cols(h)].astype(f32) * inverse
        gl[h] = scaled.astype(bf16)
        high, low = split(lead[h] * scaled)
        xx[h] = mm_tn(q_rows, high) + mm_tn(q_rows, low)
        return 0

    lax.fori_loop(0, heads, scaled_part, 0)

    @pl.when(me == 0)
    def _():
        s_in[...] = jnp.zeros_like(s_in)

    @pl.when(me == n - 1)
    def _():
        c_in[...] = jnp.zeros_like(c_in)

    per_head = HEAD // CHUNK

    def piece(ref, c):
        start = pl.multiple_of(lax.rem(c, per_head) * CHUNK, CHUNK)
        return ref.at[c // per_head, pl.ds(start, CHUNK), :]

    def onward(out, landing, send_sem, recv_sem, c, peer):
        return pltpu.make_async_remote_copy(
            src_ref=piece(out, c),
            dst_ref=piece(landing, c),
            send_sem=send_sem.at[c],
            recv_sem=recv_sem.at[c],
            device_id={"ctx": peer},
            device_id_type=MESH,
        )

    right, left = lax.rem(me + 1, n), lax.rem(me + n - 1, n)
    lag = 2 * me - (n - 1)
    f_first = jnp.clip(lag * HOP, 0, chunks)
    b_first = jnp.clip(-lag * HOP, 0, chunks)

    def pass_on(c, has_in, has_out, peer, add, landing, out, send_sem, recv_sem):
        copy = onward(out, landing, send_sem, recv_sem, c, peer)

        @pl.when(has_in)
        def _():
            copy.wait_recv()

        @pl.when(has_out)
        def _():
            factor = p_rows[pl.ds(c // per_head, 1), :]
            piece(out, c)[...] = piece(landing, c)[...] * factor + piece(add, c)[...]
            copy.start()

    def turn(s, _):
        cf = s - f_first
        cb = s - b_first

        @pl.when(jnp.logical_and(cf >= 0, cf < chunks))
        def _():
            pass_on(cf, me > 0, me < n - 1, right, yy, s_in, s_out, f_send, f_recv)

        @pl.when(jnp.logical_and(cb >= 0, cb < chunks))
        def _():
            pass_on(cb, me < n - 1, me > 0, left, xx, c_in, c_out, b_send, b_recv)

        return 0

    lax.fori_loop(0, 2 * chunks, turn, 0)

    def carried_part(h, _):
        q_rows, k_rows = qr[h], kr[h]
        high, low = split(s_in[h])
        carried = mm(q_rows, high) + mm(q_rows, low)
        inverse = rden[h]
        begin = lead[h]
        output = (num[h] + begin * carried) * inverse
        given = do[:, head_cols(h)].astype(f32)
        slant = -jnp.sum(given * output, axis=1, keepdims=True)
        slant = jnp.broadcast_to(slant, (tokens, HEAD)) * inverse
        scaled = gl[h]
        vh = v[:, head_cols(h)]
        mixed = mm_nt(scaled, vh) + jnp.concatenate([slant, slant], axis=1)
        mixed = (mixed * decay[h]).astype(bf16)
        keys_in = jnp.broadcast_to(send2[pl.ds(h, 1), :], (tokens, HEAD))
        from_state = mm_nt(scaled, high) + slant * keys_in
        query = mm(mixed, k_rows) + begin * from_state
        dq[:, head_cols(h)] = (qs[:, head_cols(h)].astype(f32) * query).astype(bf16)
        gf[pl.ds(h, 1), :] = jnp.sum(q_rows.astype(f32) * (begin * slant), axis=0, keepdims=True)
        high, low = split(c_in[h])
        end = tail[h]
        num[h] = mm_tn(mixed, q_rows) + end * (mm_nt(vh, high) + mm_nt(vh, low))
        value = mm_tn(wl[h], scaled) + end * (mm(k_rows, high) + mm(k_rows, low))
        dv[:, head_cols(h)] = value.astype(bf16)
        return 0

    lax.fori_loop(0, heads, carried_part, 0)
    ag2[me] = gf[...]
    start_gather(gf, ag2, s2_send, s2_recv)
    end_gather(gf, ag2, s2_send, s2_recv)

    def carry_back(i, state):
        at = n - 1 - i
        new = ag2[at] + ag1[at][heads : 2 * heads, :] * state
        return jnp.where(at > me, new, state)

    send2[...] = lax.fori_loop(0, n, carry_back, jnp.zeros((heads, HEAD), f32))

    def keys_part(h, _):
        vector = jnp.broadcast_to(send2[pl.ds(h, 1), :], (tokens, HEAD))
        key = num[h] + tail[h] * vector
        dk[:, head_cols(h)] = (ks[:, head_cols(h)].astype(f32) * key).astype(bf16)
        return 0

    lax.fori_loop(0, heads, keys_part, 0)
    sent_gather(*first)
    sent_gather(gf, ag2, s2_send, s2_recv)

    @pl.when(me < n - 1)
    def _():
        def one(c, _):
            onward(s_out, s_in, f_send, f_recv, c, right).wait_send()
            return 0

        lax.fori_loop(0, chunks, one, 0)

    @pl.when(me > 0)
    def _():
        def one(c, _):
            onward(c_out, c_in, b_send, b_recv, c, left).wait_send()
            return 0

        lax.fori_loop(0, chunks, one, 0)


def attention(qw, kw, v, do, gate, qs, ks):
    tokens, width = v.shape
    heads = width // HEAD
    n = lax.axis_size("ctx")
    chunks = heads * HEAD // CHUNK
    flat = jax.ShapeDtypeStruct((tokens, width), bf16)
    vm = pl.BlockSpec(memory_space=pltpu.VMEM)
    by_head = lambda a, b, t: pltpu.VMEM((heads, a, b), t)
    return pl.pallas_call(
        functools.partial(attention_kernel, n, heads, tokens),
        out_shape=(flat, flat, flat),
        in_specs=[vm] * 7,
        out_specs=(vm, vm, vm),
        scratch_shapes=[
            by_head(HEAD, tokens, bf16),
            by_head(tokens, HEAD, bf16),
            by_head(tokens, HEAD, bf16),
            by_head(tokens, HEAD, f32),
            by_head(tokens, HEAD, f32),
            by_head(tokens, tokens, bf16),
            by_head(tokens, HEAD, f32),
            by_head(tokens, HEAD, f32),
            by_head(tokens, HEAD, bf16),
            pltpu.VMEM((heads, HEAD), f32),
            by_head(tokens, tokens, f32),
            pltpu.VMEM((8, 128), f32),
            by_head(HEAD, HEAD, f32),
            by_head(HEAD, HEAD, f32),
            by_head(HEAD, HEAD, f32),
            by_head(HEAD, HEAD, f32),
            by_head(HEAD, HEAD, f32),
            by_head(HEAD, HEAD, f32),
            pltpu.VMEM((2 * heads, HEAD), f32),
            pltpu.VMEM((n, 2 * heads, HEAD), f32),
            pltpu.VMEM((heads, HEAD), f32),
            pltpu.VMEM((n, heads, HEAD), f32),
            pltpu.VMEM((heads, HEAD), f32),
            pltpu.SemaphoreType.DMA((n,)),
            pltpu.SemaphoreType.DMA((n,)),
            pltpu.SemaphoreType.DMA((n,)),
            pltpu.SemaphoreType.DMA((n,)),
            pltpu.SemaphoreType.DMA((chunks,)),
            pltpu.SemaphoreType.DMA((chunks,)),
            pltpu.SemaphoreType.DMA((chunks,)),
            pltpu.SemaphoreType.DMA((chunks,)),
        ],
        compiler_params=pltpu.CompilerParams(
            collective_id=0, has_side_effects=True, vmem_limit_bytes=40 << 20
        ),
        name="attention",
    )(qw, kw, v, do, gate, qs, ks)


def partial_kernel(
    slots, columns, tokens, pattern, xw, dv, out, xu, lhs, rhs
):
    half = BLK // 2
    words = xw.shape[0]
    step = 64

    def open_bits(i, _):
        at = pl.multiple_of(i * step, step)
        spread = jnp.broadcast_to(xw[pl.ds(at, step), :][:, None, :], (step, 8, tokens))
        shifts = 2 * lax.broadcasted_iota(jnp.int32, spread.shape, 1)
        even = jnp.bitwise_and(jnp.right_shift(spread, shifts), 1)
        odd = jnp.bitwise_and(jnp.right_shift(spread, shifts + 1), 1)
        to = pl.ds(pl.multiple_of(at * 8, step * 8), step * 8)
        xu[to, 0:tokens] = even.reshape(step * 8, tokens).astype(f32).astype(bf16)
        xu[to, tokens : 2 * tokens] = odd.reshape(step * 8, tokens).astype(f32).astype(bf16)
        return 0

    lax.fori_loop(0, words // step, open_bits, 0)

    def one_head(h, _):
        pair = dv[:, pl.ds(pl.multiple_of(h * HEAD, HEAD), HEAD)].astype(f32)
        turned = pltpu.roll(pair, BLK, axis=1)
        left = lax.broadcasted_iota(jnp.int32, pair.shape, 1) < BLK
        zero = jnp.zeros_like(pair)
        for k in range(2):
            upper, lower = (pair, turned) if k == 0 else (turned, pair)
            rhs[0:tokens, :] = jnp.where(left, upper, zero).astype(bf16)
            rhs[tokens : 2 * tokens, :] = jnp.where(left, zero, lower).astype(bf16)
            j = 2 * h + k
            for s in range(slots):
                block = pl.multiple_of(pattern[j, s] * half, half)
                lhs[s * half : (s + 1) * half, :] = xu[pl.ds(block, half), :]
            result = mm(lhs[...], rhs[...])
            for s in range(slots):
                out[s, j] = result[s * half : (s + 1) * half, :]
        return 0

    lax.fori_loop(0, columns // 2, one_head, 0)


def partials(xw, dv, pattern):
    words, tokens = xw.shape
    columns, slots = pattern.shape
    half = BLK // 2
    vm = pl.BlockSpec(memory_space=pltpu.VMEM)
    return pl.pallas_call(
        functools.partial(partial_kernel, slots, columns, tokens),
        out_shape=jax.ShapeDtypeStruct((slots, columns, half, HEAD), f32),
        in_specs=[pl.BlockSpec(memory_space=pltpu.SMEM), vm, vm],
        out_specs=vm,
        scratch_shapes=[
            pltpu.VMEM((words * 8, 2 * tokens), bf16),
            pltpu.VMEM((slots * half, 2 * tokens), bf16),
            pltpu.VMEM((2 * tokens, HEAD), bf16),
        ],
        compiler_params=pltpu.CompilerParams(vmem_limit_bytes=32 << 20),
        name="partials",
    )(pattern, xw, dv)


def sum_kernel(
    nz, columns, half,
    part, out,
    zbuf, ybuf, abuf, bbuf, mine, theirs,
    zs, zr, ys, yr, as_, ar, bs, br, es, er,
):
    ctx = lax.axis_index("ctx")
    dp = lax.axis_index("dp")
    z = lax.rem(ctx, nz)
    y_hi = ctx // nz
    y = 2 * y_hi + dp
    ny = 4
    first = columns // 2
    quarter = columns // 4

    def at_z(k):
        return {"ctx": y_hi * nz + lax.rem(z + k + nz, nz)}

    def at_y(k):
        other = lax.rem(y + k + ny, ny)
        return {"dp": lax.rem(other, 2), "ctx": (other // 2) * nz + z}

    barrier = pltpu.get_barrier_semaphore()
    partners = [at_z(k) for k in range(1, nz)] + [at_y(k) for k in range(1, ny)]
    for device in partners:
        pl.semaphore_signal(barrier, inc=1, device_id=device, device_id_type=MESH)
    pl.semaphore_wait(barrier, len(partners))

    def copy(src, dst, send, recv, device):
        return pltpu.make_async_remote_copy(
            src_ref=src, dst_ref=dst, send_sem=send, recv_sem=recv,
            device_id=device, device_id_type=MESH,
        )

    zsub, ysub = 4, 4
    zc = first // zsub

    def z_slot(direction, k):
        if direction == 0:
            return lax.rem(z - 1 - k + 2 * nz, nz)
        return nz + lax.rem(z + 1 + k, nz)

    def z_copy(direction, k, c):
        if k == 0:
            src = part.at[z_slot(direction, 0), pl.ds(c * zc, zc)]
        else:
            src = zbuf.at[direction, k - 1, pl.ds(c * zc, zc)]
        return copy(
            src, zbuf.at[direction, k, pl.ds(c * zc, zc)],
            zs.at[direction, k, c], zr.at[direction, k, c],
            at_z(1 if direction == 0 else -1),
        )

    def z_take(direction, k, c):
        z_copy(direction, k, c).wait_recv()
        where = (direction, k, pl.ds(c * zc, zc))
        own = part[z_slot(direction, k + 1), pl.ds(c * zc, zc)]
        zbuf[where] = zbuf[where] + own

    def y_place(direction, k, c):
        step = -1 - k if direction == 0 else 1 + k
        to = lax.rem(y + step + 2 * ny, ny)
        slot = (to // 2) * nz + direction * (nz // 2) + c
        return slot, pl.multiple_of(first + quarter * lax.rem(to, 2), quarter)

    def y_copy(direction, k, c):
        if k == 0:
            slot, col = y_place(direction, 0, c)
            src = part.at[slot, pl.ds(col, quarter)]
        else:
            src = ybuf.at[k - 1, direction * (nz // 2) + c]
        return copy(
            src, ybuf.at[k, direction * (nz // 2) + c],
            ys.at[direction, k, c], yr.at[direction, k, c],
            at_y(1 if direction == 0 else -1),
        )

    def y_take(direction, k, c):
        y_copy(direction, k, c).wait_recv()
        slot, col = y_place(direction, k + 1, c)
        where = (k, direction * (nz // 2) + c)
        ybuf[where] = ybuf[where] + part[slot, pl.ds(col, quarter)]

    for c in range(max(zsub, ysub)):
        for direction in (0, 1):
            if c < zsub:
                z_copy(direction, 0, c).start()
            if c < ysub:
                y_copy(direction, 0, c).start()

    events = []
    for k in range(nz - 1):
        for c in range(zsub):
            events.append((k + c / zsub, 0, k, c))
    for k in range(ny - 1):
        for c in range(ysub):
            events.append((2 * k + 2 * c / ysub + 0.9, 1, k, c))
    events.sort()
    for _, kind, k, c in events:
        for direction in (0, 1):
            if kind == 0:
                z_take(direction, k, c)
                if k < nz - 2:
                    z_copy(direction, k + 1, c).start()
            else:
                y_take(direction, k, c)
                if k < ny - 2:
                    y_copy(direction, k + 1, c).start()

    def a_copy(k):
        to = lax.rem(y + k, ny)
        col = pl.multiple_of(quarter * lax.rem(to, 2), quarter)
        return copy(
            zbuf.at[to // 2, nz - 2, pl.ds(col, quarter)], abuf.at[k],
            as_.at[k], ar.at[k], at_y(k),
        )

    def b_copy(k):
        return copy(
            ybuf.at[ny - 2, lax.rem(z + k, nz)], bbuf.at[k], bs.at[k], br.at[k], at_z(k)
        )

    a_copies = [a_copy(k) for k in range(1, ny)]
    b_copies = [b_copy(k) for k in range(1, nz)]
    for c in a_copies + b_copies:
        c.start()
    col = pl.multiple_of(quarter * dp, quarter)
    mine[0] = zbuf[y_hi, nz - 2, pl.ds(col, quarter)]
    mine[1] = ybuf[ny - 2, z]
    for k, c in enumerate(a_copies):
        c.wait_recv()
        mine[0] = mine[0] + abuf[k + 1]
    for k, c in enumerate(b_copies):
        c.wait_recv()
        mine[1] = mine[1] + bbuf[k + 1]
    swap = copy(mine, theirs, es.at[0], er.at[0], {"dp": 1 - dp})
    swap.start()
    swap.wait_recv()

    for part_at in range(2):
        own = mine[part_at]
        other = theirs[part_at]
        low = jnp.where(dp == 0, own, other)
        high = jnp.where(dp == 0, other, own)
        out[2 * part_at * quarter : (2 * part_at + 1) * quarter] = low
        out[(2 * part_at + 1) * quarter : (2 * part_at + 2) * quarter] = high

    swap.wait_send()
    for c in a_copies + b_copies:
        c.wait_send()
    for direction in (0, 1):
        for k in range(nz - 1):
            for c in range(zsub):
                z_copy(direction, k, c).wait_send()
        for k in range(ny - 1):
            for c in range(ysub):
                y_copy(direction, k, c).wait_send()


def sum_parts(part):
    slots, columns, half, lanes = part.shape
    nz = lax.axis_size("ctx") // 2
    ny = 4
    vm = pl.BlockSpec(memory_space=pltpu.VMEM)
    dma = pltpu.SemaphoreType.DMA
    return pl.pallas_call(
        functools.partial(sum_kernel, nz, columns, half),
        out_shape=jax.ShapeDtypeStruct((columns, half, lanes), f32),
        in_specs=[vm],
        out_specs=vm,
        scratch_shapes=[
            pltpu.VMEM((2, nz - 1, columns // 2, half, lanes), f32),
            pltpu.VMEM((ny - 1, nz, columns // 4, half, lanes), f32),
            pltpu.VMEM((ny, columns // 4, half, lanes), f32),
            pltpu.VMEM((nz, columns // 4, half, lanes), f32),
            pltpu.VMEM((2, columns // 4, half, lanes), f32),
            pltpu.VMEM((2, columns // 4, half, lanes), f32),
            dma((2, nz - 1, 4)), dma((2, nz - 1, 4)),
            dma((2, ny - 1, 4)), dma((2, ny - 1, 4)),
            dma((ny,)), dma((ny,)), dma((nz,)), dma((nz,)), dma((1,)), dma((1,)),
        ],
        compiler_params=pltpu.CompilerParams(
            collective_id=1, has_side_effects=True, vmem_limit_bytes=32 << 20
        ),
        name="sum_parts",
    )(part)


def per_device(
    input_spikes, query_spikes, key_spikes, values, query_slope, key_slope, grad_out, log_gate, pattern
):
    query_grad, key_grad, value_low = attention(
        query_spikes, key_spikes, values, grad_out, log_gate, query_slope, key_slope
    )
    part = partials(input_spikes, value_low, pattern)
    summed = sum_parts(part)
    return (query_grad, key_grad, summed.reshape(1, pattern.shape[0], BLK * BLK))


def solution(mesh):
    column = P("tensor", ("dp", "ctx"))
    token = P(("dp", "ctx"), "tensor")
    in_specs = (
        P(None, ("dp", "ctx")), column, column, token, token, token, token, column, P("tensor", None)
    )
    return jax.shard_map(
        per_device,
        mesh=mesh,
        in_specs=in_specs,
        out_specs=(token, token, P("ctx", "tensor", None)),
        check_vma=False,
    )
```

time: 717 us -> 165 us (0.23)
  waiting for transfers between devices: 367 us -> 0 us
  Pallas kernels: 0 us -> 153 us
  blocking collectives: 119 us -> 0 us
  matrix products: 92.2 us -> 0 us
  other arithmetic: 54.8 us -> 0 us
  local copies, waits for them, and re-layouts: 57.3 us -> 10.6 us
  between operations: 14.8 us -> 0.68 us
    reduce_scatter x1 -> x0, waiting for transfers between devices: 204 us -> none  [per_device(): lax.psum_scatter(partial_value.reshape(lax.axis_size('ctx') * row_share,...]
    pallas_call x0 -> x3, Pallas kernels: none -> 153 us  [the longest x1 100 us: attention(): pl.pallas_call(functools.partial(attention_kernel, n, heads, tokens), out...]
    all_gather x2 -> x0, waiting for transfers between devices: 130 us -> none  [entering(): everything = jax.tree.map(lambda part: lax.all_gather(part, axis), value)]
    dot_general x99 -> x0, matrix products: 92.2 us -> none  [the longest x8 14.1 us: second_phase(): lax.dot_general(weights_low, scaled_low, dims_of(0, 0), preferred_element...]
    all_gather x2 -> x0, blocking collectives: 74.6 us -> none  [entering(): everything = jax.tree.map(lambda part: lax.all_gather(part, axis), value)]
    unnamed x1 -> x0, blocking collectives: 44.3 us -> none
    select_n x65 -> x0, other arithmetic: 39.8 us -> none  [the longest x64 39.8 us: turn(): return jax.tree.map(lambda a, b: jnp.where(reached, a, b), new, before)]
    psum x1 -> x0, waiting for transfers between devices: 32.8 us -> none  [per_device(): value_grad = lax.psum(reduced, 'dp')]
  transfers between devices with their start and end apart: 4 -> 0, of which waited for: 4 -> 0; matrix products, arithmetic and copies ran while one was open for 4% -> 0% of each run, Pallas kernels for 0% -> 0%
where the time goes in v1:
time: 165 us; the launch traced here: 164 us
  Pallas kernels  153 us (93%)
  local copies, waits for them, and re-layouts  10.6 us (6%)
    pallas_call x1, Pallas kernels, attention(): pl.pallas_call(functools.partial(attention_kernel, n, heads, tokens), out...  100 us
    pallas_call x1, Pallas kernels, sum_parts(): pl.pallas_call(functools.partial(sum_kernel, nz, columns, half), out_shap...  46.7 us
    unnamed x20, local copies, waits for them, and re-layouts  9.85 us
    pallas_call x1, Pallas kernels, partials(): pl.pallas_call(functools.partial(partial_kernel, slots, columns, tokens),...  6.18 us

profile of v1, /device:TPU:14, one launch (start us, length us, event | category | flops | bytes accessed | tf_op | source)
XLA Modules:
  0.0 164.2 jit_solution(4603069332564602057)
XLA Ops:
  0.6 0.0 copy-start
  0.6 1.0 copy-done
  1.7 0.0 copy-start.1
  1.7 1.0 copy-done.1
  2.7 0.0 copy-start.2
  2.7 1.0 copy-done.2
  3.8 0.0 copy-start.3
  3.8 1.0 copy-done.3
  4.8 0.0 copy-start.5
  4.8 0.8 copy-done.5
  5.6 0.0 copy-start.6
  5.6 0.8 copy-done.6
  6.5 0.0 copy-start.7
  6.5 0.7 copy-done.7
  7.2 100.1 %attention.1 = (bf16[256,1024]{1,0:T(8,128)(2,1)S(1)}, bf16[256,1024]{1,0:T(8,128)(2,1)S(1)}, bf16[256,1024]{1,0:T(8,128)(2,1)S(1)}) custom-call(s32[64,256]{1,0:T(8,128)S(1)} %copy-done.5, s32[64,256]{1,0:T(8,128)S(1)} %copy-done.6, bf16[256,1024]{1,0:T(8,128)(2,1)S(1)} %copy-done, bf16[256,1024]{1,0:T(8,128)(2,1)S(1)} %copy-done.1, ...), custom_call_target="tpu_custom_call" | custom-call | tf_op jit(solution)/shard_map/attention/pallas_call | solution.py:339
  107.3 0.0 copy-start.4
  107.3 1.0 copy-done.4
  108.3 0.0 copy-start.8
  108.3 0.7 copy-done.8
  109.0 6.2 %partials.1.part = f32[16,16,32,128]{3,2,1,0:T(8,128)S(1)} custom-call(s32[16,16]{1,0:T(8,128)S(1)} %copy-done.8, s32[512,256]{1,0:T(8,128)S(1)} %copy-done.4, bf16[256,1024]{1,0:T(8,128)(2,1)S(1)} %get-tuple-element.8.dv), custom_call_target="tpu_custom_call" | custom-call | tf_op jit(solution)/shard_map/partials/pallas_call | solution.py:430
  115.2 46.7 %sum_parts.1 = f32[16,32,128]{2,1,0:T(8,128)S(1)} custom-call(f32[16,16,32,128]{3,2,1,0:T(8,128)S(1)} %partials.1.part), custom_call_target="tpu_custom_call" | custom-call | tf_op jit(solution)/shard_map/sum_parts/pallas_call | solution.py:610
  161.9 0.8 reshape.9
  162.6 0.8 copy.14
  163.4 0.8 copy.15
Async XLA Ops:
  0.6 1.0 copy-start
  1.7 1.0 copy-start.1
  2.7 1.0 copy-start.2
  3.8 1.0 copy-start.3
  4.8 0.8 copy-start.5
  5.6 0.8 copy-start.6
  6.5 0.7 copy-start.7
  107.3 1.0 copy-start.4
  108.3 0.7 copy-start.8

commit v2 on v0

v2 whole, which is shorter than its diff:
```python
import functools
import types

import jax
import jax.numpy as jnp
from jax import lax
from jax.experimental import pallas as pl
from jax.experimental.pallas import tpu as pltpu
from jax.sharding import PartitionSpec as P

HEAD = 128
BLK = 64
SEL = 16
MESH = pl.DeviceIdType.MESH
CHUNK = 32
HOP = 5
CROSS = 8
f32 = jnp.float32
bf16 = jnp.bfloat16


def mm(a, b):
    return lax.dot_general(a, b, (((1,), (0,)), ((), ())), preferred_element_type=f32)


def mm_nt(a, b):
    return lax.dot_general(a, b, (((1,), (1,)), ((), ())), preferred_element_type=f32)


def mm_tn(a, b):
    return lax.dot_general(a, b, (((0,), (0,)), ((), ())), preferred_element_type=f32)


def split(a):
    high = a.astype(bf16)
    return high, (a - high.astype(f32)).astype(bf16)


def mm_exact_left(a, b):
    high, low = split(b)
    return mm(a, high) + mm(a, low)


def bits_of(words, tokens):
    spread = jnp.broadcast_to(words[:, None, :], (HEAD // 16, 16, tokens))
    shifts = lax.broadcasted_iota(jnp.int32, spread.shape, 1)
    flags = jnp.bitwise_and(jnp.right_shift(spread, shifts), 1)
    return flags.reshape(HEAD, tokens).astype(f32).astype(bf16)


def copy_to(src, dst, send, recv, device):
    return pltpu.make_async_remote_copy(
        src_ref=src, dst_ref=dst, send_sem=send, recv_sem=recv,
        device_id=device, device_id_type=MESH,
    )


def kernel(n, heads, tokens, columns, slots, names, pattern, *refs):
    r = types.SimpleNamespace(**dict(zip(names, refs)))
    me = lax.axis_index("ctx")
    dp = lax.axis_index("dp")
    nz, ny = n // 2, 4
    z, y_hi = lax.rem(me, nz), me // nz
    y = 2 * y_hi + dp
    chunks = heads * HEAD // CHUNK
    per_head = HEAD // CHUNK
    half = BLK // 2

    def at_ctx(k):
        return {"ctx": k}

    def at_z(k):
        return {"ctx": y_hi * nz + lax.rem(z + k + nz, nz)}

    def at_y(k):
        other = lax.rem(y + k + ny, ny)
        return {"dp": lax.rem(other, 2), "ctx": (other // 2) * nz + z}

    barrier = pltpu.get_barrier_semaphore()

    def greet(i, _):
        pl.semaphore_signal(
            barrier, inc=1, device_id=at_ctx(lax.rem(me + i, n)), device_id_type=MESH
        )
        return 0

    lax.fori_loop(1, n, greet, 0)
    for k in (1, 3):
        pl.semaphore_signal(barrier, inc=1, device_id=at_y(k), device_id_type=MESH)

    loads = {}
    for i, name in enumerate(("gate", "kw", "qw", "v", "do", "xw", "qs", "ks")):
        loads[name] = pltpu.make_async_copy(
            getattr(r, name + "_h"), getattr(r, name), r.in_sem.at[i]
        )
        loads[name].start()

    rows = lax.broadcasted_iota(jnp.int32, (tokens, tokens), 0)
    cols = lax.broadcasted_iota(jnp.int32, (tokens, tokens), 1)
    lower = (rows >= cols).astype(f32)
    hi = lax.Precision.HIGHEST
    loads["gate"].wait()
    gates = r.gate[...]
    r.send1[heads : 2 * heads, :] = jnp.exp(
        jnp.broadcast_to(jnp.sum(gates, axis=1, keepdims=True), (heads, HEAD))
    )
    loads["kw"].wait()

    def head_cols(h):
        return pl.ds(pl.multiple_of(h * HEAD, HEAD), HEAD)

    def head_words(h):
        return pl.ds(pl.multiple_of(h * (HEAD // 16), HEAD // 16), HEAD // 16)

    def sums(h, _):
        keys = bits_of(r.kw[head_words(h), :], tokens)
        r.kc[h] = keys
        key_rows = keys.T
        r.kr[h] = key_rows
        spread = jnp.broadcast_to(r.gate[pl.ds(h, 1), :], (HEAD, tokens))
        run = lax.dot_general(
            lower, spread, (((1,), (1,)), ((), ())), precision=hi, preferred_element_type=f32
        )
        r.lead[h] = run
        last = jnp.broadcast_to(run[tokens - 1 : tokens, :], (tokens, HEAD))
        end = jnp.exp(last - run)
        r.tail[h] = end
        r.send1[pl.ds(h, 1), :] = jnp.sum(key_rows.astype(f32) * end, axis=0, keepdims=True)
        return 0

    lax.fori_loop(0, heads, sums, 0)
    r.ag1[me] = r.send1[...]
    pl.semaphore_wait(barrier, n + 1)

    def gather(send, target, send_sem, recv_sem, i):
        peer = lax.rem(me + i, n)
        return copy_to(send, target.at[me], send_sem.at[i], recv_sem.at[me], at_ctx(peer))

    def arrival(send, target, send_sem, recv_sem, i):
        peer = lax.rem(me + i, n)
        return copy_to(send, target.at[peer], send_sem.at[i], recv_sem.at[peer], at_ctx(peer))

    def start_gather(*which):
        def one(i, _):
            gather(*which, i).start()
            return 0

        lax.fori_loop(1, n, one, 0)

    def end_gather(*which):
        def one(i, _):
            arrival(*which, i).wait_recv()
            return 0

        lax.fori_loop(1, n, one, 0)

    def sent_gather(*which):
        def one(i, _):
            gather(*which, i).wait_send()
            return 0

        lax.fori_loop(1, n, one, 0)

    first_gather = (r.send1, r.ag1, r.s1_send, r.s1_recv)
    second_gather = (r.gf, r.ag2, r.s2_send, r.s2_recv)
    start_gather(*first_gather)
    loads["qw"].wait()
    loads["v"].wait()

    def local_part(h, _):
        r.qr[h] = bits_of(r.qw[head_words(h), :], tokens).T
        run = r.lead[h]
        run_wide = jnp.concatenate([run, run], axis=1)
        run_row = lax.dot_general(
            jnp.broadcast_to(r.gate[pl.ds(h, 1), :], (8, tokens)), lower,
            (((1,), (1,)), ((), ())), precision=hi, preferred_element_type=f32,
        )[0:1, :]
        spread = run_wide - jnp.broadcast_to(run_row, (tokens, tokens))
        mask = jnp.where(rows >= cols, jnp.exp(jnp.minimum(spread, 0.0)), 0.0)
        r.decay[h] = mask
        weights = mm(r.qr[h], r.kc[h]) * mask
        low = weights.astype(bf16)
        r.wl[h] = low
        vh = r.v[:, head_cols(h)]
        r.num[h] = mm(low, vh)
        r.rden[h] = jnp.broadcast_to(jnp.sum(weights, axis=1, keepdims=True), (tokens, HEAD))
        r.yy[h] = mm_exact_left(r.kc[h], r.tail[h] * vh.astype(f32))
        r.lead[h] = jnp.exp(run)
        return 0

    lax.fori_loop(0, heads, local_part, 0)
    end_gather(*first_gather)

    def carry_keys(i, state):
        keys, down, up = state
        item = r.ag1[i]
        factor = item[heads : 2 * heads, :]
        keys = jnp.where(i < me, factor * keys + item[0:heads, :], keys)
        down = jnp.where(jnp.logical_and(i > me, i < nz), down * factor, down)
        up = jnp.where(jnp.logical_and(i < me, i >= nz), up * factor, up)
        return keys, down, up

    ones = jnp.ones((heads, HEAD), f32)
    keys, down, up = lax.fori_loop(0, n, carry_keys, (jnp.zeros((heads, HEAD), f32), ones, ones))
    r.keys_in[...] = keys
    r.down[...] = jnp.where(y_hi == 0, down, 0.0)
    r.up[...] = jnp.where(y_hi == 1, up, 0.0)
    loads["do"].wait()

    def scaled_part(h, _):
        keys_in = jnp.broadcast_to(r.keys_in[pl.ds(h, 1), :], (HEAD, HEAD))
        high, low = split(keys_in)
        q_rows = r.qr[h]
        met = mm_nt(q_rows, high) + mm_nt(q_rows, low)
        inverse = 1.0 / (1.0 + r.rden[h] + r.lead[h] * met)
        r.rden[h] = inverse
        scaled = r.do[:, head_cols(h)].astype(f32) * inverse
        r.gl[h] = scaled.astype(bf16)
        high, low = split(r.lead[h] * scaled)
        r.xx[h] = mm_tn(q_rows, high) + mm_tn(q_rows, low)
        return 0

    lax.fori_loop(0, heads, scaled_part, 0)
    loads["xw"].wait()

    @pl.when(z == 0)
    def _():
        r.s_in[...] = jnp.zeros_like(r.s_in)

    @pl.when(z == nz - 1)
    def _():
        r.c_in[...] = jnp.zeros_like(r.c_in)

    def piece(ref, c):
        start = pl.multiple_of(lax.rem(c, per_head) * CHUNK, CHUNK)
        return ref.at[c // per_head, pl.ds(start, CHUNK), :]

    def entry(line, group):
        near = jnp.where(line == 1, nz - 1, 0)
        return jnp.where(group == 0, near, nz - 1 - near)

    def line_copy(forward, c):
        out, landing, send, recv, step = (
            (r.s_out, r.s_in, r.f_send, r.f_recv, 1)
            if forward
            else (r.c_out, r.c_in, r.b_send, r.b_recv, -1)
        )
        return copy_to(piece(out, c), piece(landing, c), send.at[c], recv.at[c], at_z(step))

    def cross_copy(forward, c):
        out, send = (r.s_out, r.f_send) if forward else (r.c_out, r.b_send)
        line = 1 if forward else 0
        at = line * nz + entry(line, c // (chunks // 2))
        return copy_to(piece(out, c), piece(r.total, c), send.at[c], r.t_recv.at[c], at_ctx(at))

    def pass_line(forward, c):
        last = (nz - 1) if forward else 0
        has_in = z > 0 if forward else z < nz - 1
        onward = z != last
        crossing = jnp.logical_and(z == last, y_hi == (0 if forward else 1))
        landing, out, add = (r.s_in, r.s_out, r.yy) if forward else (r.c_in, r.c_out, r.xx)

        @pl.when(has_in)
        def _():
            line_copy(forward, c).wait_recv()

        @pl.when(jnp.logical_or(onward, crossing))
        def _():
            factor = r.send1[pl.ds(heads + c // per_head, 1), :]
            piece(out, c)[...] = piece(landing, c)[...] * factor + piece(add, c)[...]

        @pl.when(onward)
        def _():
            line_copy(forward, c).start()

        @pl.when(crossing)
        def _():
            cross_copy(forward, c).start()

    def total_copy(c, step):
        send = r.t_send_down if step < 0 else r.t_send_up
        return copy_to(piece(r.total, c), piece(r.total, c), send.at[c], r.t_recv.at[c], at_z(step))

    def distances(group):
        e = entry(y_hi, group)
        return lax.rem(e - z + nz, nz), lax.rem(z - e + nz, nz)

    def pass_total(group, c):
        below, above = distances(group)
        total_copy(c, -1).wait_recv()

        @pl.when(below < nz // 2)
        def _():
            total_copy(c, -1).start()

        @pl.when(above < nz // 2 - 1)
        def _():
            total_copy(c, 1).start()

    step_words = r.xw.shape[0] // heads

    def side_part(h):
        r.dvl[h] = mm_tn(r.wl[h], r.gl[h])
        at = pl.multiple_of(h * step_words, step_words)
        spread = jnp.broadcast_to(
            r.xw[pl.ds(at, step_words), :][:, None, :], (step_words, 8, tokens)
        )
        shifts = 2 * lax.broadcasted_iota(jnp.int32, spread.shape, 1)
        even = jnp.bitwise_and(jnp.right_shift(spread, shifts), 1)
        odd = jnp.bitwise_and(jnp.right_shift(spread, shifts + 1), 1)
        count = step_words * 8 // half
        to = pl.ds(h * count, count)
        r.xu[to, :, 0:tokens] = even.reshape(count, half, tokens).astype(f32).astype(bf16)
        r.xu[to, :, tokens : 2 * tokens] = odd.reshape(count, half, tokens).astype(f32).astype(bf16)

    f_off = z * HOP
    b_off = (nz - 1 - z) * HOP
    t_off = []
    for group in range(2):
        below, above = distances(group)
        t_off.append(
            (nz - 1) * HOP + CROSS + jnp.minimum(below, above) * HOP + group * (chunks // 2)
        )
    side_off = jnp.where(z < nz // 2, 0, chunks)
    steps = (nz - 1) * HOP + CROSS + nz // 2 * HOP + chunks

    def turn(s, _):
        for group in range(2):
            ct = s - t_off[group]

            @pl.when(jnp.logical_and(ct >= 0, ct < chunks // 2))
            def _():
                pass_total(group, ct + group * (chunks // 2))

        cb = s - b_off

        @pl.when(jnp.logical_and(cb >= 0, cb < chunks))
        def _():
            pass_line(False, cb)

        cf = s - f_off

        @pl.when(jnp.logical_and(cf >= 0, cf < chunks))
        def _():
            pass_line(True, cf)

        cs = s - side_off

        @pl.when(jnp.logical_and(cs >= 0, cs < heads))
        def _():
            side_part(cs)

        return 0

    lax.fori_loop(0, steps, turn, 0)

    def product_part(h, _):
        adjoint = r.c_in[h] + r.down[pl.ds(h, 1), :] * r.total[h]
        r.c_in[h] = adjoint
        high, low = split(adjoint)
        k_rows = r.kr[h]
        value = r.dvl[h] + r.tail[h] * (mm(k_rows, high) + mm(k_rows, low))
        pair = value.astype(bf16).astype(f32)
        turned = pltpu.roll(pair, BLK, axis=1)
        left = lax.broadcasted_iota(jnp.int32, pair.shape, 1) < BLK
        zero = jnp.zeros_like(pair)
        for k in range(2):
            upper, under = (pair, turned) if k == 0 else (turned, pair)
            r.rhs[0:tokens, :] = jnp.where(left, upper, zero).astype(bf16)
            r.rhs[tokens : 2 * tokens, :] = jnp.where(left, zero, under).astype(bf16)
            j = 2 * h + k
            for s in range(slots):
                r.lhs[s * half : (s + 1) * half, :] = r.xu[pattern[j, s]]
            result = mm(r.lhs[...], r.rhs[...])
            for s in range(slots):
                r.part[s, j] = result[s * half : (s + 1) * half, :]
        return 0

    def carried_part(h):
        q_rows, k_rows = r.qr[h], r.kr[h]
        high, low = split(r.s_in[h] + r.up[pl.ds(h, 1), :] * r.total[h])
        carried = mm(q_rows, high) + mm(q_rows, low)
        inverse = r.rden[h]
        begin = r.lead[h]
        output = (r.num[h] + begin * carried) * inverse
        given = r.do[:, head_cols(h)].astype(f32)
        slant = -jnp.sum(given * output, axis=1, keepdims=True)
        slant = jnp.broadcast_to(slant, (tokens, HEAD)) * inverse
        scaled = r.gl[h]
        vh = r.v[:, head_cols(h)]
        mixed = mm_nt(scaled, vh) + jnp.concatenate([slant, slant], axis=1)
        mixed = (mixed * r.decay[h]).astype(bf16)
        keys_in = jnp.broadcast_to(r.keys_in[pl.ds(h, 1), :], (tokens, HEAD))
        from_state = mm_nt(scaled, high) + slant * keys_in
        query = mm(mixed, k_rows) + begin * from_state
        r.dq[:, head_cols(h)] = (r.qs[:, head_cols(h)].astype(f32) * query).astype(bf16)
        r.gf[pl.ds(h, 1), :] = jnp.sum(q_rows.astype(f32) * (begin * slant), axis=0, keepdims=True)
        high, low = split(r.c_in[h])
        r.num[h] = mm_tn(mixed, q_rows) + r.tail[h] * (mm_nt(vh, high) + mm_nt(vh, low))

    def second_start():
        r.ag2[me] = r.gf[...]
        start_gather(*second_gather)

    def keys_end():
        end_gather(*second_gather)

        def carry_back(i, state):
            at = n - 1 - i
            new = r.ag2[at] + r.ag1[at][heads : 2 * heads, :] * state
            return jnp.where(at > me, new, state)

        r.keys_in[...] = lax.fori_loop(0, n, carry_back, jnp.zeros((heads, HEAD), f32))

        def keys_part(h, _):
            vector = jnp.broadcast_to(r.keys_in[pl.ds(h, 1), :], (tokens, HEAD))
            key = r.num[h] + r.tail[h] * vector
            r.dk[:, head_cols(h)] = (r.ks[:, head_cols(h)].astype(f32) * key).astype(bf16)
            return 0

        lax.fori_loop(0, heads, keys_part, 0)

    part, zbuf, ybuf = r.part, r.zbuf, r.ybuf
    first, quarter = columns // 2, columns // 4
    zsub = ysub = 4
    zc = first // zsub

    def z_slot(direction, k):
        if direction == 0:
            return lax.rem(z - 1 - k + 2 * nz, nz)
        return nz + lax.rem(z + 1 + k, nz)

    def z_copy(direction, k, c):
        if k == 0:
            src = part.at[z_slot(direction, 0), pl.ds(c * zc, zc)]
        else:
            src = zbuf.at[direction, k - 1, pl.ds(c * zc, zc)]
        return copy_to(
            src, zbuf.at[direction, k, pl.ds(c * zc, zc)],
            r.zs.at[direction, k, c], r.zr.at[direction, k, c],
            at_z(1 if direction == 0 else -1),
        )

    def z_take(direction, k, c):
        z_copy(direction, k, c).wait_recv()
        where = (direction, k, pl.ds(c * zc, zc))
        zbuf[where] = zbuf[where] + part[z_slot(direction, k + 1), pl.ds(c * zc, zc)]

    def y_place(direction, k, c):
        step = -1 - k if direction == 0 else 1 + k
        to = lax.rem(y + step + 2 * ny, ny)
        slot = (to // 2) * nz + direction * (nz // 2) + c
        return slot, pl.multiple_of(first + quarter * lax.rem(to, 2), quarter)

    def y_copy(direction, k, c):
        if k == 0:
            slot, col = y_place(direction, 0, c)
            src = part.at[slot, pl.ds(col, quarter)]
        else:
            src = ybuf.at[k - 1, direction * (nz // 2) + c]
        return copy_to(
            src, ybuf.at[k, direction * (nz // 2) + c],
            r.ys.at[direction, k, c], r.yr.at[direction, k, c],
            at_y(1 if direction == 0 else -1),
        )

    def y_take(direction, k, c):
        y_copy(direction, k, c).wait_recv()
        slot, col = y_place(direction, k + 1, c)
        where = (k, direction * (nz // 2) + c)
        ybuf[where] = ybuf[where] + part[slot, pl.ds(col, quarter)]

    lax.fori_loop(0, heads // 2, product_part, 0)
    for c in range(zsub):
        for direction in (0, 1):
            z_copy(direction, 0, c).start()
    lax.fori_loop(heads // 2, heads, product_part, 0)
    for c in range(ysub):
        for direction in (0, 1):
            y_copy(direction, 0, c).start()
    loads["qs"].wait()
    loads["ks"].wait()

    events = []
    for k in range(nz - 1):
        for c in range(zsub):
            events.append((k + c / zsub, 0, k, c))
    for k in range(ny - 1):
        for c in range(ysub):
            events.append((2 * k + 2 * c / ysub + 0.9, 1, k, c))
    for h in range(heads):
        events.append((0.3 + 4.0 * h / heads, 2, h, 0))
    events.append((4.3, 3, 0, 0))
    events.sort()
    for _, kind, k, c in events:
        if kind == 2:
            carried_part(k)
            continue
        if kind == 3:
            second_start()
            continue
        for direction in (0, 1):
            if kind == 0:
                z_take(direction, k, c)
                if k < nz - 2:
                    z_copy(direction, k + 1, c).start()
            else:
                y_take(direction, k, c)
                if k < ny - 2:
                    y_copy(direction, k + 1, c).start()

    def a_copy(k):
        to = lax.rem(y + k, ny)
        col = pl.multiple_of(quarter * lax.rem(to, 2), quarter)
        return copy_to(
            zbuf.at[to // 2, nz - 2, pl.ds(col, quarter)], r.abuf.at[k],
            r.as_.at[k], r.ar.at[k], at_y(k),
        )

    def b_copy(k):
        return copy_to(
            ybuf.at[ny - 2, lax.rem(z + k, nz)], r.bbuf.at[k], r.bs.at[k], r.br.at[k], at_z(k)
        )

    a_copies = [a_copy(k) for k in range(1, ny)]
    b_copies = [b_copy(k) for k in range(1, nz)]
    for c in b_copies + a_copies:
        c.start()
    keys_end()
    mine, theirs = r.mine, r.theirs
    col = pl.multiple_of(quarter * dp, quarter)
    mine[0] = zbuf[y_hi, nz - 2, pl.ds(col, quarter)]
    mine[1] = ybuf[ny - 2, z]
    for k, c in enumerate(a_copies):
        c.wait_recv()
        mine[0] = mine[0] + r.abuf[k + 1]
    for k, c in enumerate(b_copies):
        c.wait_recv()
        mine[1] = mine[1] + r.bbuf[k + 1]
    swap = copy_to(mine, theirs, r.es.at[0], r.er.at[0], {"dp": 1 - dp})
    swap.start()
    swap.wait_recv()

    for k in range(2):
        own, other = mine[k], theirs[k]
        r.out[2 * k * quarter : (2 * k + 1) * quarter] = jnp.where(dp == 0, own, other)
        r.out[(2 * k + 1) * quarter : (2 * k + 2) * quarter] = jnp.where(dp == 0, other, own)

    swap.wait_send()
    for c in a_copies + b_copies:
        c.wait_send()
    for direction in (0, 1):
        for k in range(nz - 1):
            for c in range(zsub):
                z_copy(direction, k, c).wait_send()
        for k in range(ny - 1):
            for c in range(ysub):
                y_copy(direction, k, c).wait_send()
    sent_gather(*first_gather)
    sent_gather(*second_gather)

    @pl.when(jnp.logical_or(z < nz - 1, y_hi == 0))
    def _():
        def one(c, _):
            line_copy(True, c).wait_send()
            return 0

        lax.fori_loop(0, chunks, one, 0)

    @pl.when(jnp.logical_or(z > 0, y_hi == 1))
    def _():
        def one(c, _):
            line_copy(False, c).wait_send()
            return 0

        lax.fori_loop(0, chunks, one, 0)

    for group in range(2):
        below, above = distances(group)
        span = (group * (chunks // 2), (group + 1) * (chunks // 2))

        @pl.when(below < nz // 2)
        def _():
            def one(c, _):
                total_copy(c, -1).wait_send()
                return 0

            lax.fori_loop(*span, one, 0)

        @pl.when(above < nz // 2 - 1)
        def _():
            def one(c, _):
                total_copy(c, 1).wait_send()
                return 0

            lax.fori_loop(*span, one, 0)


def per_device(xw, qw, kw, v, qs, ks, do, gate, pattern):
    tokens, width = v.shape
    heads = width // HEAD
    words = xw.shape[0]
    columns, slots = pattern.shape
    n = lax.axis_size("ctx")
    nz, ny = n // 2, 4
    chunks = heads * HEAD // CHUNK
    half = BLK // 2
    flat = jax.ShapeDtypeStruct((tokens, width), bf16)
    vmem, dma = pltpu.VMEM, pltpu.SemaphoreType.DMA
    scratch = dict(
        gate=vmem(gate.shape, f32),
        kw=vmem(kw.shape, jnp.int32),
        qw=vmem(qw.shape, jnp.int32),
        v=vmem(v.shape, bf16),
        do=vmem(v.shape, bf16),
        xw=vmem(xw.shape, jnp.int32),
        qs=vmem(v.shape, bf16),
        ks=vmem(v.shape, bf16),
        in_sem=dma((8,)),
        kc=vmem((heads, HEAD, tokens), bf16),
        kr=vmem((heads, tokens, HEAD), bf16),
        qr=vmem((heads, tokens, HEAD), bf16),
        gl=vmem((heads, tokens, HEAD), bf16),
        wl=vmem((heads, tokens, tokens), bf16),
        decay=vmem((heads, tokens, tokens), f32),
        xu=vmem((words * 8 // half, half, 2 * tokens), bf16),
        lhs=vmem((slots * half, 2 * tokens), bf16),
        rhs=vmem((2 * tokens, HEAD), bf16),
        part=vmem((slots, columns, half, HEAD), f32),
        send1=vmem((2 * heads, HEAD), f32),
        ag1=vmem((n, 2 * heads, HEAD), f32),
        ag2=vmem((n, heads, HEAD), f32),
        zbuf=vmem((2, nz - 1, columns // 2, half, HEAD), f32),
        ybuf=vmem((ny - 1, nz, columns // 4, half, HEAD), f32),
        abuf=vmem((ny, columns // 4, half, HEAD), f32),
        bbuf=vmem((nz, columns // 4, half, HEAD), f32),
        mine=vmem((2, columns // 4, half, HEAD), f32),
        theirs=vmem((2, columns // 4, half, HEAD), f32),
        zs=dma((2, nz - 1, 4)),
        zr=dma((2, nz - 1, 4)),
        ys=dma((2, ny - 1, 4)),
        yr=dma((2, ny - 1, 4)),
        as_=dma((ny,)),
        ar=dma((ny,)),
        bs=dma((nz,)),
        br=dma((nz,)),
        es=dma((1,)),
        er=dma((1,)),
    )
    for name in ("lead", "tail", "num", "rden", "dvl"):
        scratch[name] = vmem((heads, tokens, HEAD), f32)
    for name in ("yy", "s_in", "s_out", "xx", "c_in", "c_out", "total"):
        scratch[name] = vmem((heads, HEAD, HEAD), f32)
    for name in ("gf", "keys_in", "down", "up"):
        scratch[name] = vmem((heads, HEAD), f32)
    for name in ("s1_send", "s1_recv", "s2_send", "s2_recv"):
        scratch[name] = dma((n,))
    for name in ("f_send", "f_recv", "b_send", "b_recv", "t_recv", "t_send_up", "t_send_down"):
        scratch[name] = dma((chunks,))
    arguments = ("xw_h", "qw_h", "kw_h", "v_h", "do_h", "gate_h", "qs_h", "ks_h")
    names = arguments + ("dq", "dk", "out") + tuple(scratch)
    whole = pl.BlockSpec(memory_space=pltpu.VMEM)
    dq, dk, out = pl.pallas_call(
        functools.partial(kernel, n, heads, tokens, columns, slots, names),
        out_shape=(flat, flat, jax.ShapeDtypeStruct((columns, half, HEAD), f32)),
        in_specs=[pl.BlockSpec(memory_space=pltpu.SMEM)] + [pl.BlockSpec(memory_space=pl.ANY)] * 8,
        out_specs=(whole, whole, whole),
        scratch_shapes=list(scratch.values()),
        compiler_params=pltpu.CompilerParams(
            collective_id=0, has_side_effects=True, vmem_limit_bytes=60 << 20
        ),
        name="layer",
    )(pattern, xw, qw, kw, v, do, gate, qs, ks)
    return dq, dk, out.reshape(1, columns, BLK * BLK)


def solution(mesh):
    column = P("tensor", ("dp", "ctx"))
    token = P(("dp", "ctx"), "tensor")
    in_specs = (
        P(None, ("dp", "ctx")), column, column, token, token, token, token, column, P("tensor", None)
    )
    return jax.shard_map(
        per_device,
        mesh=mesh,
        in_specs=in_specs,
        out_specs=(token, token, P("ctx", "tensor", None)),
        check_vma=False,
    )
```

time: 717 us -> 132 us (0.18)
  waiting for transfers between devices: 367 us -> 0 us
  Pallas kernels: 0 us -> 127 us
  blocking collectives: 119 us -> 0 us
  matrix products: 92.2 us -> 0 us
  other arithmetic: 54.8 us -> 0 us
  local copies, waits for them, and re-layouts: 57.3 us -> 3.79 us
  between operations: 14.8 us -> 0.65 us
    reduce_scatter x1 -> x0, waiting for transfers between devices: 204 us -> none  [per_device(): lax.psum_scatter(partial_value.reshape(lax.axis_size('ctx') * row_share,...]
    all_gather x2 -> x0, waiting for transfers between devices: 130 us -> none  [entering(): everything = jax.tree.map(lambda part: lax.all_gather(part, axis), value)]
    pallas_call x0 -> x1, Pallas kernels: none -> 127 us  [per_device(): pl.pallas_call(functools.partial(kernel, n, heads, tokens, columns, slots...]
    dot_general x99 -> x0, matrix products: 92.2 us -> none  [the longest x8 14.1 us: second_phase(): lax.dot_general(weights_low, scaled_low, dims_of(0, 0), preferred_element...]
    all_gather x2 -> x0, blocking collectives: 74.6 us -> none  [entering(): everything = jax.tree.map(lambda part: lax.all_gather(part, axis), value)]
    unnamed x1 -> x0, blocking collectives: 44.3 us -> none
    select_n x65 -> x0, other arithmetic: 39.8 us -> none  [the longest x64 39.8 us: turn(): return jax.tree.map(lambda a, b: jnp.where(reached, a, b), new, before)]
    psum x1 -> x0, waiting for transfers between devices: 32.8 us -> none  [per_device(): value_grad = lax.psum(reduced, 'dp')]
  transfers between devices with their start and end apart: 4 -> 0, of which waited for: 4 -> 0; matrix products, arithmetic and copies ran while one was open for 4% -> 0% of each run, Pallas kernels for 0% -> 0%
where the time goes in v2:
time: 132 us
  Pallas kernels  127 us (96%)
  local copies, waits for them, and re-layouts  3.79 us (3%)
    pallas_call x1, Pallas kernels, per_device(): pl.pallas_call(functools.partial(kernel, n, heads, tokens, columns, slots...  127 us

profile of v2, /device:TPU:14, one launch (start us, length us, event | category | flops | bytes accessed | tf_op | source)
XLA Modules:
  0.0 131.9 jit_solution(3867642036540739196)
XLA Ops:
  0.6 127.5 %layer.1 = (bf16[256,1024]{1,0:T(8,128)(2,1)}, bf16[256,1024]{1,0:T(8,128)(2,1)}, f32[16,32,128]{2,1,0:T(8,128)}) custom-call(s32[16,16]{1,0:T(8,128)} %pattern.1, s32[512,256]{1,0:T(8,128)} %refs_0_.1, s32[64,256]{1,0:T(8,128)} %refs_1_.1, s32[64,256]{1,0:T(8,128)} %refs_2_.1, bf16[256,1024]{1,0:T(8,128)(2,1)} %refs_3_.1, bf16[256,1024]{1,0:T(8,128)(2,1)} %refs_4_.1, ...), custom_call_target="tpu_custom_call" | custom-call | tf_op jit(solution)/shard_map/layer/pallas_call | solution.py:663
  128.1 0.0 copy-start.1
  128.1 1.8 %reshape.9 = f32[1,16,4096]{2,1,0:T(8,128)} reshape(f32[16,32,128]{2,1,0:T(8,128)} %get-tuple-element.8) | data formatting | bytes 524288 | tf_op jit(solution)/shard_map/reshape | solution.py:674
  129.9 0.0 copy-done.1
  129.9 0.0 copy-start
  129.9 0.8 copy.14
  130.7 0.4 copy-done
  131.1 0.8 copy.15
Async XLA Ops:
  128.1 1.8 %copy-start.1 = (bf16[256,1024]{1,0:T(8,128)(2,1)S(1)}, bf16[256,1024]{1,0:T(8,128)(2,1)}, u32[]{:S(2)}) copy-start(bf16[256,1024]{1,0:T(8,128)(2,1)} %get-tuple-element.12) | copy-start | bytes 1572868
  129.9 1.2 copy-start

commit v3 on v2

--- a/solution.py
+++ b/solution.py
@@ -13,8 +13,8 @@
 SEL = 16
 MESH = pl.DeviceIdType.MESH
 CHUNK = 32
-HOP = 5
-CROSS = 8
+HOP = 8
+CROSS = 12
 f32 = jnp.float32
 bf16 = jnp.bfloat16
 
@@ -34,6 +34,12 @@
 def split(a):
     high = a.astype(bf16)
     return high, (a - high.astype(f32)).astype(bf16)
+
+
+def split3(a):
+    high = a.astype(bf16)
+    rest = a - high.astype(f32)
+    return (high, *split(rest))
 
 
 def mm_exact_left(a, b):
@@ -97,12 +103,16 @@
 
     rows = lax.broadcasted_iota(jnp.int32, (tokens, tokens), 0)
     cols = lax.broadcasted_iota(jnp.int32, (tokens, tokens), 1)
-    lower = (rows >= cols).astype(f32)
-    hi = lax.Precision.HIGHEST
+    lower = jnp.where(rows >= cols, 1.0, 0.0)
+    lower_bits = lower.astype(bf16)
     loads["gate"].wait()
     gates = r.gate[...]
     r.send1[heads : 2 * heads, :] = jnp.exp(
         jnp.broadcast_to(jnp.sum(gates, axis=1, keepdims=True), (heads, HEAD))
+    )
+    r.run_rows[...] = lax.dot_general(
+        gates, lower, (((1,), (1,)), ((), ())),
+        precision=lax.Precision.HIGHEST, preferred_element_type=f32,
     )
     loads["kw"].wait()
 
@@ -118,9 +128,7 @@
         key_rows = keys.T
         r.kr[h] = key_rows
         spread = jnp.broadcast_to(r.gate[pl.ds(h, 1), :], (HEAD, tokens))
-        run = lax.dot_general(
-            lower, spread, (((1,), (1,)), ((), ())), precision=hi, preferred_element_type=f32
-        )
+        run = sum(mm_nt(lower_bits, part) for part in split3(spread))
         r.lead[h] = run
         last = jnp.broadcast_to(run[tokens - 1 : tokens, :], (tokens, HEAD))
         end = jnp.exp(last - run)
@@ -171,11 +179,7 @@
         r.qr[h] = bits_of(r.qw[head_words(h), :], tokens).T
         run = r.lead[h]
         run_wide = jnp.concatenate([run, run], axis=1)
-        run_row = lax.dot_general(
-            jnp.broadcast_to(r.gate[pl.ds(h, 1), :], (8, tokens)), lower,
-            (((1,), (1,)), ((), ())), precision=hi, preferred_element_type=f32,
-        )[0:1, :]
-        spread = run_wide - jnp.broadcast_to(run_row, (tokens, tokens))
+        spread = run_wide - jnp.broadcast_to(r.run_rows[pl.ds(h, 1), :], (tokens, tokens))
         mask = jnp.where(rows >= cols, jnp.exp(jnp.minimum(spread, 0.0)), 0.0)
         r.decay[h] = mask
         weights = mm(r.qr[h], r.kc[h]) * mask
@@ -543,8 +547,11 @@
 
     for k in range(2):
         own, other = mine[k], theirs[k]
-        r.out[2 * k * quarter : (2 * k + 1) * quarter] = jnp.where(dp == 0, own, other)
-        r.out[(2 * k + 1) * quarter : (2 * k + 2) * quarter] = jnp.where(dp == 0, other, own)
+        low, high = 2 * k * quarter, (2 * k + 1) * quarter
+        r.blocks[low : low + quarter] = jnp.where(dp == 0, own, other)
+        r.blocks[high : high + quarter] = jnp.where(dp == 0, other, own)
+    for k in range(half):
+        r.out[:, k * HEAD : (k + 1) * HEAD] = r.blocks[:, k, :]
 
     swap.wait_send()
     for c in a_copies + b_copies:
@@ -636,6 +643,8 @@
         bbuf=vmem((nz, columns // 4, half, HEAD), f32),
         mine=vmem((2, columns // 4, half, HEAD), f32),
         theirs=vmem((2, columns // 4, half, HEAD), f32),
+        blocks=vmem((columns, half, HEAD), f32),
+        run_rows=vmem((heads, tokens), f32),
         zs=dma((2, nz - 1, 4)),
         zr=dma((2, nz - 1, 4)),
         ys=dma((2, ny - 1, 4)),
@@ -662,7 +671,7 @@
     whole = pl.BlockSpec(memory_space=pltpu.VMEM)
     dq, dk, out = pl.pallas_call(
         functools.partial(kernel, n, heads, tokens, columns, slots, names),
-        out_shape=(flat, flat, jax.ShapeDtypeStruct((columns, half, HEAD), f32)),
+        out_shape=(flat, flat, jax.ShapeDtypeStruct((columns, BLK * BLK), f32)),
         in_specs=[pl.BlockSpec(memory_space=pltpu.SMEM)] + [pl.BlockSpec(memory_space=pl.ANY)] * 8,
         out_specs=(whole, whole, whole),
         scratch_shapes=list(scratch.values()),

time: 132 us -> 127 us (0.962)
  Pallas kernels: 127 us -> 122 us
    pallas_call x1, Pallas kernels: 127 us -> 122 us  [per_device(): pl.pallas_call(functools.partial(kernel, n, heads, tokens, columns, slots...]
    reshape x1 -> x0, local copies, waits for them, and re-layouts: 1.76 us -> none  [per_device(): return (dq, dk, out.reshape(1, columns, BLK * BLK))]
    unnamed x6 -> x7, local copies, waits for them, and re-layouts: 2.03 us -> 3.72 us
where the time goes in v3:
time: 127 us; the launch traced here: 126 us
  Pallas kernels  122 us (96%)
  local copies, waits for them, and re-layouts  3.72 us (3%)
    pallas_call x1, Pallas kernels, per_device(): pl.pallas_call(functools.partial(kernel, n, heads, tokens, columns, slots...  122 us
    unnamed x7, local copies, waits for them, and re-layouts  3.72 us

profile of v3, /device:TPU:14, one launch (start us, length us, event | category | flops | bytes accessed | tf_op | source)
XLA Modules:
  0.0 125.9 jit_solution(3160607589667694757)
XLA Ops:
  0.6 121.5 %layer.1 = (bf16[256,1024]{1,0:T(8,128)(2,1)}, bf16[256,1024]{1,0:T(8,128)(2,1)}, f32[16,4096]{1,0:T(8,128)}) custom-call(s32[16,16]{1,0:T(8,128)} %pattern.1, s32[512,256]{1,0:T(8,128)} %refs_0_.1, s32[64,256]{1,0:T(8,128)} %refs_1_.1, s32[64,256]{1,0:T(8,128)} %refs_2_.1, bf16[256,1024]{1,0:T(8,128)(2,1)} %refs_3_.1, bf16[256,1024]{1,0:T(8,128)(2,1)} %refs_4_.1, ...), custom_call_target="tpu_custom_call" | custom-call | tf_op jit(solution)/shard_map/layer/pallas_call | solution.py:672
  122.2 0.0 copy-start
  122.2 1.9 %copy.15 = bf16[256,1024]{1,0:T(8,128)(2,1)} copy(bf16[256,1024]{1,0:T(8,128)(2,1)} %get-tuple-element.12) | data formatting | bytes 1048576
  124.1 0.0 copy-done
  124.1 0.0 copy-start.1
  124.1 0.8 copy.16
  124.9 0.3 copy-done.1
  125.2 0.7 copy.17
Async XLA Ops:
  122.2 1.9 %copy-start = (bf16[256,1024]{1,0:T(8,128)(2,1)S(1)}, bf16[256,1024]{1,0:T(8,128)(2,1)}, u32[]{:S(2)}) copy-start(bf16[256,1024]{1,0:T(8,128)(2,1)} %get-tuple-element.13) | copy-start | bytes 1572868
  124.1 1.1 copy-start.1

commit v4 on v3

--- a/solution.py
+++ b/solution.py
@@ -68,6 +68,8 @@
     nz, ny = n // 2, 4
     z, y_hi = lax.rem(me, nz), me // nz
     y = 2 * y_hi + dp
+    turned = jnp.where(y_hi == 1, z, nz - 1 - z)
+    middle = nz // 2 - 1
     chunks = heads * HEAD // CHUNK
     per_head = HEAD // CHUNK
     half = BLK // 2
@@ -207,6 +209,7 @@
     ones = jnp.ones((heads, HEAD), f32)
     keys, down, up = lax.fori_loop(0, n, carry_keys, (jnp.zeros((heads, HEAD), f32), ones, ones))
     r.keys_in[...] = keys
+    r.mix[...] = down * up
     r.down[...] = jnp.where(y_hi == 0, down, 0.0)
     r.up[...] = jnp.where(y_hi == 1, up, 0.0)
     loads["do"].wait()
@@ -231,6 +234,10 @@
     def _():
         r.s_in[...] = jnp.zeros_like(r.s_in)
 
+    @pl.when(turned == 0)
+    def _():
+        r.u_in[...] = jnp.zeros_like(r.u_in)
+
     @pl.when(z == nz - 1)
     def _():
         r.c_in[...] = jnp.zeros_like(r.c_in)
@@ -240,7 +247,7 @@
         return ref.at[c // per_head, pl.ds(start, CHUNK), :]
 
     def entry(line, group):
-        near = jnp.where(line == 1, nz - 1, 0)
+        near = jnp.where(line == 1, nz // 2, nz // 2 - 1)
         return jnp.where(group == 0, near, nz - 1 - near)
 
     def line_copy(forward, c):
@@ -252,33 +259,59 @@
         return copy_to(piece(out, c), piece(landing, c), send.at[c], recv.at[c], at_z(step))
 
     def cross_copy(forward, c):
-        out, send = (r.s_out, r.f_send) if forward else (r.c_out, r.b_send)
         line = 1 if forward else 0
         at = line * nz + entry(line, c // (chunks // 2))
-        return copy_to(piece(out, c), piece(r.total, c), send.at[c], r.t_recv.at[c], at_ctx(at))
+        return copy_to(
+            piece(r.u_out, c), piece(r.total, c), r.u_send.at[c], r.t_recv.at[c], at_ctx(at)
+        )
+
+    def early_copy(c):
+        step = jnp.where(y_hi == 1, 1, -1)
+        return copy_to(
+            piece(r.u_out, c), piece(r.u_in, c), r.u_send.at[c], r.u_recv.at[c], at_z(step)
+        )
+
+    def join(c, ref):
+        factor = r.mix[pl.ds(c // per_head, 1), :]
+        piece(r.u_out, c)[...] = piece(r.u_in, c)[...] + factor * piece(ref, c)[...]
+
+    def pass_early(c):
+        @pl.when(turned > 0)
+        def _():
+            early_copy(c).wait_recv()
+
+        @pl.when(y_hi == 1)
+        def _():
+            join(c, r.xx)
+
+        @pl.when(y_hi == 0)
+        def _():
+            join(c, r.yy)
+
+        early_copy(c).start()
 
     def pass_line(forward, c):
         last = (nz - 1) if forward else 0
         has_in = z > 0 if forward else z < nz - 1
         onward = z != last
-        crossing = jnp.logical_and(z == last, y_hi == (0 if forward else 1))
+        crossing = jnp.logical_and(turned == middle, y_hi == (0 if forward else 1))
         landing, out, add = (r.s_in, r.s_out, r.yy) if forward else (r.c_in, r.c_out, r.xx)
 
         @pl.when(has_in)
         def _():
             line_copy(forward, c).wait_recv()
 
-        @pl.when(jnp.logical_or(onward, crossing))
+        @pl.when(onward)
         def _():
             factor = r.send1[pl.ds(heads + c // per_head, 1), :]
             piece(out, c)[...] = piece(landing, c)[...] * factor + piece(add, c)[...]
 
-        @pl.when(onward)
-        def _():
             line_copy(forward, c).start()
 
         @pl.when(crossing)
         def _():
+            early_copy(c).wait_recv()
+            join(c, out)
             cross_copy(forward, c).start()
 
     def total_copy(c, step):
@@ -323,10 +356,15 @@
     for group in range(2):
         below, above = distances(group)
         t_off.append(
-            (nz - 1) * HOP + CROSS + jnp.minimum(below, above) * HOP + group * (chunks // 2)
-        )
-    side_off = jnp.where(z < nz // 2, 0, chunks)
-    steps = (nz - 1) * HOP + CROSS + nz // 2 * HOP + chunks
+            nz // 2 * HOP + CROSS + jnp.minimum(below, above) * HOP + group * (chunks // 2)
+        )
+    u_off = turned * HOP
+    side_off = jnp.where(
+        z >= nz - 2,
+        chunks + 1 + (nz - 1 - z) * HOP,
+        jnp.where(jnp.logical_and(y_hi == 1, z <= 1), chunks + 2 + z * (HOP // 2), 0),
+    )
+    steps = nz * HOP + CROSS + chunks
 
     def turn(s, _):
         for group in range(2):
@@ -341,6 +379,12 @@
         @pl.when(jnp.logical_and(cb >= 0, cb < chunks))
         def _():
             pass_line(False, cb)
+
+        cu = s - u_off
+
+        @pl.when(jnp.logical_and(turned < middle, jnp.logical_and(cu >= 0, cu < chunks)))
+        def _():
+            pass_early(cu)
 
         cf = s - f_off
 
@@ -566,7 +610,15 @@
     sent_gather(*first_gather)
     sent_gather(*second_gather)
 
-    @pl.when(jnp.logical_or(z < nz - 1, y_hi == 0))
+    @pl.when(turned <= middle)
+    def _():
+        def one(c, _):
+            early_copy(c).wait_send()
+            return 0
+
+        lax.fori_loop(0, chunks, one, 0)
+
+    @pl.when(z < nz - 1)
     def _():
         def one(c, _):
             line_copy(True, c).wait_send()
@@ -574,7 +626,7 @@
 
         lax.fori_loop(0, chunks, one, 0)
 
-    @pl.when(jnp.logical_or(z > 0, y_hi == 1))
+    @pl.when(z > 0)
     def _():
         def one(c, _):
             line_copy(False, c).wait_send()
@@ -658,13 +710,13 @@
     )
     for name in ("lead", "tail", "num", "rden", "dvl"):
         scratch[name] = vmem((heads, tokens, HEAD), f32)
-    for name in ("yy", "s_in", "s_out", "xx", "c_in", "c_out", "total"):
+    for name in ("yy", "s_in", "s_out", "xx", "c_in", "c_out", "total", "u_in", "u_out"):
         scratch[name] = vmem((heads, HEAD, HEAD), f32)
-    for name in ("gf", "keys_in", "down", "up"):
+    for name in ("gf", "keys_in", "down", "up", "mix"):
         scratch[name] = vmem((heads, HEAD), f32)
     for name in ("s1_send", "s1_recv", "s2_send", "s2_recv"):
         scratch[name] = dma((n,))
-    for name in ("f_send", "f_recv", "b_send", "b_recv", "t_recv", "t_send_up", "t_send_down"):
+    for name in ("f_send", "f_recv", "b_send", "b_recv", "t_recv", "t_send_up", "t_send_down", "u_send", "u_recv"):
         scratch[name] = dma((chunks,))
     arguments = ("xw_h", "qw_h", "kw_h", "v_h", "do_h", "gate_h", "qs_h", "ks_h")
     names = arguments + ("dq", "dk", "out") + tuple(scratch)

time: 127 us -> 132 us (1.039)
  Pallas kernels: 122 us -> 127 us
    pallas_call x1, Pallas kernels: 122 us -> 127 us  [per_device(): pl.pallas_call(functools.partial(kernel, n, heads, tokens, columns, slots...]
where the time goes in v4:
time: 132 us
  Pallas kernels  127 us (96%)
  local copies, waits for them, and re-layouts  3.72 us (3%)
    pallas_call x1, Pallas kernels, per_device(): pl.pallas_call(functools.partial(kernel, n, heads, tokens, columns, slots...  127 us
    unnamed x7, local copies, waits for them, and re-layouts  3.72 us

profile of v4, /device:TPU:14, one launch (start us, length us, event | category | flops | bytes accessed | tf_op | source)
XLA Modules:
  0.0 131.7 jit_solution(7539759940869656607)
XLA Ops:
  0.6 127.3 %layer.1 = (bf16[256,1024]{1,0:T(8,128)(2,1)}, bf16[256,1024]{1,0:T(8,128)(2,1)}, f32[16,4096]{1,0:T(8,128)}) custom-call(s32[16,16]{1,0:T(8,128)} %pattern.1, s32[512,256]{1,0:T(8,128)} %refs_0_.1, s32[64,256]{1,0:T(8,128)} %refs_1_.1, s32[64,256]{1,0:T(8,128)} %refs_2_.1, bf16[256,1024]{1,0:T(8,128)(2,1)} %refs_3_.1, bf16[256,1024]{1,0:T(8,128)(2,1)} %refs_4_.1, ...), custom_call_target="tpu_custom_call" | custom-call | tf_op jit(solution)/shard_map/layer/pallas_call | solution.py:724
  127.9 0.0 copy-start
  128.0 1.9 %copy.15 = bf16[256,1024]{1,0:T(8,128)(2,1)} copy(bf16[256,1024]{1,0:T(8,128)(2,1)} %get-tuple-element.12) | data formatting | bytes 1048576
  129.9 0.0 copy-done
  129.9 0.0 copy-start.1
  129.9 0.8 copy.16
  130.7 0.3 copy-done.1
  131.0 0.7 copy.17
Async XLA Ops:
  127.9 1.9 %copy-start = (bf16[256,1024]{1,0:T(8,128)(2,1)S(1)}, bf16[256,1024]{1,0:T(8,128)(2,1)}, u32[]{:S(2)}) copy-start(bf16[256,1024]{1,0:T(8,128)(2,1)} %get-tuple-element.13) | copy-start | bytes 1572868
  129.9 1.1 copy-start.1

commit v5 on v4

--- a/solution.py
+++ b/solution.py
@@ -14,7 +14,7 @@
 MESH = pl.DeviceIdType.MESH
 CHUNK = 32
 HOP = 8
-CROSS = 12
+CROSS = 28
 f32 = jnp.float32
 bf16 = jnp.bfloat16
 

time: 132 us -> 132 us (level)
  no operation moved by 1% of the time
where the time goes in v5:
time: 132 us; the launch traced here: 131 us
  Pallas kernels  127 us (96%)
  local copies, waits for them, and re-layouts  3.72 us (3%)
    pallas_call x1, Pallas kernels, per_device(): pl.pallas_call(functools.partial(kernel, n, heads, tokens, columns, slots...  127 us
    unnamed x7, local copies, waits for them, and re-layouts  3.72 us

profile of v5, /device:TPU:14, one launch (start us, length us, event | category | flops | bytes accessed | tf_op | source)
XLA Modules:
  0.0 130.9 jit_solution(7556260552139418234)
XLA Ops:
  0.6 126.6 %layer.1 = (bf16[256,1024]{1,0:T(8,128)(2,1)}, bf16[256,1024]{1,0:T(8,128)(2,1)}, f32[16,4096]{1,0:T(8,128)}) custom-call(s32[16,16]{1,0:T(8,128)} %pattern.1, s32[512,256]{1,0:T(8,128)} %refs_0_.1, s32[64,256]{1,0:T(8,128)} %refs_1_.1, s32[64,256]{1,0:T(8,128)} %refs_2_.1, bf16[256,1024]{1,0:T(8,128)(2,1)} %refs_3_.1, bf16[256,1024]{1,0:T(8,128)(2,1)} %refs_4_.1, ...), custom_call_target="tpu_custom_call" | custom-call | tf_op jit(solution)/shard_map/layer/pallas_call | solution.py:724
  127.2 0.0 copy-start
  127.2 1.9 %copy.15 = bf16[256,1024]{1,0:T(8,128)(2,1)} copy(bf16[256,1024]{1,0:T(8,128)(2,1)} %get-tuple-element.12) | data formatting | bytes 1048576
  129.1 0.0 copy-done
  129.2 0.0 copy-start.1
  129.2 0.8 copy.16
  129.9 0.3 copy-done.1
  130.2 0.7 copy.17
Async XLA Ops:
  127.2 1.9 %copy-start = (bf16[256,1024]{1,0:T(8,128)(2,1)S(1)}, bf16[256,1024]{1,0:T(8,128)(2,1)}, u32[]{:S(2)}) copy-start(bf16[256,1024]{1,0:T(8,128)(2,1)} %get-tuple-element.13) | copy-start | bytes 1572868
  129.2 1.1 copy-start.1
